TPU v7x, 512 devices: a whole 4x8x8 slice. The times are simulated.
512 devices in a mesh: date: 16 (over z, y_lo), az: 32 (over y_hi, x, core).
Axes of the slice: x: 4, y: 8 (y_hi: 4, y_lo: 2; y = y_hi * 2 + y_lo), z: 8, core: 2. Of those that a mesh axis runs over, the one named last changes fastest.
Arguments:
- slc_stack: bfloat16 [2, 256, 4096, 128], P(None, 'date', 'az'), may hold values from -6 to 6
- fir_taps: float32 [256, 5], P('date'), may hold values from 0.1 to 1
- look_index: int32 [32, 16, 64], P('az', 'date'), may hold values from 0 to 1023
- shrink_level: int32 [32, 16], P('az', 'date'), may hold values from 1 to 12
- window_half: int32 [256], replicated, may hold values from 0 to 2
- basis: bfloat16 [32, 256], replicated, may hold values from -0.375 to 0.375
Outputs:
- projection: float32 [32, 2, 4096, 128], P('date', None, 'az')
Inputs may be any that keep to these rules, and one draw needn't show every extreme that they name: `look_index`: pixel numbers inside one block of 8 rows.
All inputs are finite; a program needn't handle non-finite values.
Results may differ from a plain program's by a relative error of at most 0.0048.
Values may be sent and summed in bfloat16 or wider, within the bound.
No kernel may reach another device: no remote copies, remote signals or barrier semaphores. Data moves between devices by JAX's collectives and lax.ppermute only.
A program may use at most 64 MiB of HBM per device.

v0:
```python
import jax
import jax.numpy as jnp
from jax import lax
from jax.sharding import PartitionSpec as P

NS_ITERS = 6
SMOOTH_REACH = 2


def padded_2(block, sides, width):
    for axis, dim in sides:
        count = lax.axis_size(axis)
        forward = [(i, i + 1) for i in range(count - 1)]
        backward = [(target, source) for source, target in forward]
        low = lax.ppermute(
            lax.slice_in_dim(block, block.shape[dim] - width, None, axis=dim), axis, forward
        )
        high = lax.ppermute(lax.slice_in_dim(block, 0, width, axis=dim), axis, backward)
        block = jnp.concatenate([low, block, high], axis=dim)
    return block


def complex_product(left_re, left_im, right_re, right_im):
    highest = lax.Precision.HIGHEST
    real = jnp.dot(left_re, right_re, precision=highest) - jnp.dot(
        left_im, right_im, precision=highest
    )
    imag = jnp.dot(left_re, right_im, precision=highest) + jnp.dot(
        left_im, right_re, precision=highest
    )
    return (real, imag)


def wiener_block(pixels, chosen, level):
    sample = jnp.take(pixels, chosen, axis=2)
    samp_re = sample[0]
    samp_im = sample[1]
    looks = chosen.shape[0]
    gram_re = (
        jnp.dot(samp_re, samp_re.T, preferred_element_type=jnp.float32)
        + jnp.dot(samp_im, samp_im.T, preferred_element_type=jnp.float32)
    ) / looks
    gram_im = (
        jnp.dot(samp_im, samp_re.T, preferred_element_type=jnp.float32)
        - jnp.dot(samp_re, samp_im.T, preferred_element_type=jnp.float32)
    ) / looks
    count = gram_re.shape[0]
    identity = jnp.eye(count, dtype=jnp.float32)
    level_mean = jnp.trace(gram_re) / count + 1e-06
    weight = level.astype(jnp.float32) / 16.0
    shrunk_re = (1.0 - weight) * gram_re + weight * level_mean * identity
    shrunk_im = (1.0 - weight) * gram_im
    load_re = shrunk_re + level_mean * identity
    scale = 1.0 / jnp.sqrt(jnp.sum(load_re * load_re + shrunk_im * shrunk_im))
    inv_re = identity * scale
    inv_im = jnp.zeros_like(identity)
    for step in range(NS_ITERS):
        prod_re, prod_im = complex_product(load_re, shrunk_im, inv_re, inv_im)
        inv_re, inv_im = complex_product(inv_re, inv_im, 2.0 * identity - prod_re, -prod_im)
    gain_re, gain_im = complex_product(shrunk_re, shrunk_im, inv_re, inv_im)
    gain_re = gain_re.astype(jnp.bfloat16)
    gain_im = gain_im.astype(jnp.bfloat16)
    pix_re = pixels[0]
    pix_im = pixels[1]
    out_re = jnp.dot(gain_re, pix_re, preferred_element_type=jnp.float32) - jnp.dot(
        gain_im, pix_im, preferred_element_type=jnp.float32
    )
    out_im = jnp.dot(gain_re, pix_im, preferred_element_type=jnp.float32) + jnp.dot(
        gain_im, pix_re, preferred_element_type=jnp.float32
    )
    return jnp.stack([out_re, out_im]).astype(jnp.bfloat16)


def smooth_weights(halves, reach):
    offsets = jnp.arange(-reach, reach + 1)
    inside = (jnp.abs(offsets)[None, :] <= halves[:, None]).astype(jnp.float32)
    return inside / (2 * halves + 1).astype(jnp.float32)[:, None]


def smooth_rows(rim, weights, length):
    smoothed = jnp.zeros((rim.shape[0], rim.shape[1], length, rim.shape[3]), jnp.float32)
    for offset in range(2 * SMOOTH_REACH + 1):
        smoothed = smoothed + weights[:, offset][:, None, None] * rim[
            :, :, offset : offset + length, :
        ].astype(jnp.float32)
    return smoothed.astype(jnp.bfloat16)


def on_device(slc_stack, fir_taps, look_index, shrink_level, window_half, basis):
    date_local = slc_stack.shape[1]
    rows = slc_stack.shape[2]
    columns = slc_stack.shape[3]
    groups = lax.axis_size("date")
    block_pixels = rows * columns // groups
    reach = (fir_taps.shape[1] - 1) // 2
    padded = padded_2(slc_stack, (("az", 2),), reach)
    filtered = jnp.zeros(slc_stack.shape, jnp.float32)
    for offset in range(2 * reach + 1):
        filtered = filtered + fir_taps[:, offset][:, None, None] * padded[
            :, :, offset : offset + rows, :
        ].astype(jnp.float32)
    filtered = filtered.astype(jnp.bfloat16)
    grouped = filtered.reshape(2, date_local, groups, block_pixels)
    stacked = lax.all_to_all(grouped, "date", split_axis=2, concat_axis=1, tiled=True)
    wiener = wiener_block(stacked[:, :, 0, :], look_index[0, 0], shrink_level[0, 0])
    bases = basis.shape[0]
    own_bases = bases // groups
    returned = lax.all_to_all(
        wiener[:, :, None, :], "date", split_axis=1, concat_axis=2, tiled=True
    )
    returned = returned.reshape(2, date_local, rows, columns)
    rim = padded_2(returned, (("az", 2),), SMOOTH_REACH)
    first_date = lax.axis_index("date") * date_local
    own_halves = lax.dynamic_slice_in_dim(window_half, first_date, date_local, 0)
    smoothed = smooth_rows(rim, smooth_weights(own_halves, SMOOTH_REACH), rows)
    own_basis = lax.dynamic_slice_in_dim(basis, first_date, date_local, 1)
    flat = smoothed.reshape(2, date_local, rows * columns)
    term = jnp.einsum("kt,ctp->kcp", own_basis, flat, preferred_element_type=jnp.float32)
    return lax.psum_scatter(
        term.reshape(own_bases * lax.axis_size("date"), 2, rows, columns),
        "date",
        scatter_dimension=0,
        tiled=True,
    )


def solution(mesh):
    in_specs = (
        P(None, "date", "az", None),
        P("date", None),
        P("az", "date", None),
        P("az", "date"),
        P(),
        P(),
    )
    out_specs = P("date", None, "az", None)
    return jax.shard_map(
        on_device, mesh=mesh, in_specs=in_specs, out_specs=out_specs, check_vma=False
    )
```

profile of v0, /device:TPU:1, one launch (start us, length us, event | category | flops | bytes accessed | tf_op | source)
XLA Modules:
  0.0 248.2 jit_solution(11574189538253602207)
XLA Ops:
  6.5 1.0 fusion.87
  7.5 8.7 %collective-permute-start.1 = (bf16[2,16,2,128]{3,2,1,0:T(2,128)(2,1)S(1)}, bf16[2,16,2,128]{3,2,1,0:T(2,128)(2,1)S(1)}, u32[]{:S(2)}, u32[]{:S(2)}) collective-permute-start(bf16[2,16,2,128]{3,2,1,0:T(2,128)(2,1)S(1)} %get-tuple-element.13), channel_id=1, source_target_pairs={{1,0},{2,1},{3,2},{4,3},{5,4},{6,5},{7,6},{8,7},{9,8},{10,9},{11,1... | collective-permute-start | bytes 49160 | tf_op jit(solution)/shard_map/ppermute | solution.py:18
  16.3 1.9 collective-permute-start
  18.2 0.9 slice_bitcast_fusion.8
  19.1 1.3 constant_dynamic-update-slice_fusion.1
  20.5 1.7 add_convert_fusion.1
  22.7 1.5 copy.40
  24.2 6.9 %all-to-all-start = ((bf16[2,16,16,1024]{3,1,0,2:T(8,128)(2,1)}), bf16[2,16,16,1024]{3,1,0,2:T(8,128)(2,1)S(1)}, u32[]{:S(2)}, u32[]{:S(2)}) async-start(bf16[2,16,16,1024]{3,1,0,2:T(8,128)(2,1)} %copy.40), calls=%async_computation | async-start | bytes 2097152 | tf_op jit(solution)/shard_map/all_to_all | solution.py:104
  31.9 27.7 %all-to-all-done = bf16[2,16,16,1024]{3,1,0,2:T(8,128)(2,1)S(1)} async-done(((bf16[2,16,16,1024]{3,1,0,2:T(8,128)(2,1)}), bf16[2,16,16,1024]{3,1,0,2:T(8,128)(2,1)S(1)}, u32[]{:S(2)}, u32[]{:S(2)}) %all-to-all-start) | async-done | bytes 1048608 | tf_op jit(solution)/shard_map/all_to_all | solution.py:104
  59.7 1.1 copy.42
  60.8 0.7 gather_fusion
  62.2 0.8 select_reduce_fusion
  64.1 0.9 add_reduce_fusion
  77.0 0.6 fusion.78
  86.6 2.0 copy.43
  88.7 4.0 %all-to-all-start.1 = ((bf16[2,256,1,1024]{3,0,2,1:T(2,128)(2,1)}), bf16[2,256,1,1024]{3,0,2,1:T(2,128)(2,1)S(1)}, u32[]{:S(2)}, u32[]{:S(2)}) async-start(bf16[2,256,1,1024]{3,0,2,1:T(2,128)(2,1)} %copy.43), calls=%async_computation.1 | async-start | bytes 2097152 | tf_op jit(solution)/shard_map/all_to_all | solution.py:108
  92.9 25.9 %all-to-all-done.1 = bf16[2,256,1,1024]{3,0,2,1:T(2,128)(2,1)S(1)} async-done(((bf16[2,256,1,1024]{3,0,2,1:T(2,128)(2,1)}), bf16[2,256,1,1024]{3,0,2,1:T(2,128)(2,1)S(1)}, u32[]{:S(2)}, u32[]{:S(2)}) %all-to-all-start.1) | async-done | bytes 1048608 | tf_op jit(solution)/shard_map/all_to_all | solution.py:108
  120.2 4.3 %collective-permute-start.3 = (bf16[2,16,2,128]{3,2,1,0:T(2,128)(2,1)S(1)}, bf16[2,16,2,128]{3,2,1,0:T(2,128)(2,1)S(1)}, u32[]{:S(2)}, u32[]{:S(2)}) collective-permute-start(bf16[2,16,2,128]{3,2,1,0:T(2,128)(2,1)S(1)} %get-tuple-element.7), channel_id=1, source_target_pairs={{1,0},{2,1},{3,2},{4,3},{5,4},{6,5},{7,6},{8,7},{9,8},{10,9},{11,1... | collective-permute-start | bytes 49160 | tf_op jit(solution)/shard_map/ppermute | solution.py:18
  124.7 2.3 collective-permute-start.2
  127.0 0.8 collective-permute-done.2
  127.8 1.6 add_convert_fusion
  130.0 0.7 fusion.21
  130.7 4.4 %copy.47 = f32[32,2,128,128]{3,2,1,0:T(8,128)} copy(f32[32,2,128,128]{3,0,2,1:T(8,128)S(1)} %fusion.21) | data formatting | bytes 8388608 | tf_op jit(solution)/shard_map/kt,ctp->kcp/dot_general | solution.py:118
  135.1 106.2 %reduce-scatter.2.cloned.1.call-done = f32[2,2,128,128]{3,2,1,0:T(8,128)} async-done(((f32[32,2,128,128]{3,2,1,0:T(8,128)}), f32[2,2,128,128]{3,2,1,0:T(8,128)}) %reduce-scatter.2.cloned.1.call-update) | async-done | bytes 262160 | tf_op jit(solution)/shard_map/reduce_scatter | solution.py:119
  (89 shorter events, 23.8 us)
Async XLA Ops:
  6.5 123.4 %copy-start = (bf16[32,256]{1,0:T(8,128)(2,1)S(1)}, bf16[32,256]{1,0:T(8,128)(2,1)}, u32[]{:S(2)}) copy-start(bf16[32,256]{1,0:T(8,128)(2,1)} %param.11) | copy-start | bytes 49156
  6.5 13.9 %copy-start.1 = (bf16[2,16,128,128]{3,2,1,0:T(8,128)(2,1)S(1)}, bf16[2,16,128,128]{3,2,1,0:T(8,128)(2,1)}, u32[]{:S(2)}) copy-start(bf16[2,16,128,128]{3,2,1,0:T(8,128)(2,1)} %param.6) | copy-start | bytes 3145732
  7.5 12.9 %collective-permute-start.1 = (bf16[2,16,2,128]{3,2,1,0:T(2,128)(2,1)S(1)}, bf16[2,16,2,128]{3,2,1,0:T(2,128)(2,1)S(1)}, u32[]{:S(2)}, u32[]{:S(2)}) collective-permute-start(bf16[2,16,2,128]{3,2,1,0:T(2,128)(2,1)S(1)} %get-tuple-element.13), channel_id=1, source_target_pairs={{1,0},{2,1},{3,2},{4,3},{5,4},{6,5},{7,6},{8,7},{9,8},{10,9},{11,1... | collective-permute-start | bytes 49160 | tf_op jit(solution)/shard_map/ppermute | solution.py:18
  16.3 4.2 %collective-permute-start = (bf16[2,16,2,128]{3,2,1,0:T(2,128)(2,1)S(1)}, bf16[2,16,2,128]{3,2,1,0:T(2,128)(2,1)S(1)}, u32[]{:S(2)}, u32[]{:S(2)}) collective-permute-start(bf16[2,16,2,128]{3,2,1,0:T(2,128)(2,1)S(1)} %get-tuple-element.14), channel_id=1, source_target_pairs={{0,1},{1,2},{2,3},{3,4},{4,5},{5,6},{6,7},{7,8},{8,9},{9,10},{10,1... | collective-permute-start | bytes 49160 | tf_op jit(solution)/shard_map/ppermute | solution.py:15
  22.7 9.1 %copy-start.3 = (s32[1,1,64]{2,1,0:T(1,128)S(1)}, s32[1,1,64]{2,1,0:T(1,128)}, u32[]{:S(2)}) copy-start(s32[1,1,64]{2,1,0:T(1,128)} %param.8) | copy-start | bytes 772
  24.2 35.3 %all-to-all-start = ((bf16[2,16,16,1024]{3,1,0,2:T(8,128)(2,1)}), bf16[2,16,16,1024]{3,1,0,2:T(8,128)(2,1)S(1)}, u32[]{:S(2)}, u32[]{:S(2)}) async-start(bf16[2,16,16,1024]{3,1,0,2:T(8,128)(2,1)} %copy.40), calls=%async_computation | async-start | bytes 2097152 | tf_op jit(solution)/shard_map/all_to_all | solution.py:104
  86.6 6.2 %copy-start.2 = (s32[256]{0:T(256)S(1)}, s32[256]{0:T(256)}, u32[]{:S(2)}) copy-start(s32[256]{0:T(256)} %param.10) | copy-start | bytes 3076
  88.7 30.2 %all-to-all-start.1 = ((bf16[2,256,1,1024]{3,0,2,1:T(2,128)(2,1)}), bf16[2,256,1,1024]{3,0,2,1:T(2,128)(2,1)S(1)}, u32[]{:S(2)}, u32[]{:S(2)}) async-start(bf16[2,256,1,1024]{3,0,2,1:T(2,128)(2,1)} %copy.43), calls=%async_computation.1 | async-start | bytes 2097152 | tf_op jit(solution)/shard_map/all_to_all | solution.py:108
  92.7 148.6 %reduce-scatter.2.cloned.1.call-start = ((), (), s32[]{:S(2)}) async-start(), calls=%async_computation.3 | async-start | bytes 4456448 | tf_op jit(solution)/shard_map/reduce_scatter | solution.py:119
  120.2 6.7 %collective-permute-start.3 = (bf16[2,16,2,128]{3,2,1,0:T(2,128)(2,1)S(1)}, bf16[2,16,2,128]{3,2,1,0:T(2,128)(2,1)S(1)}, u32[]{:S(2)}, u32[]{:S(2)}) collective-permute-start(bf16[2,16,2,128]{3,2,1,0:T(2,128)(2,1)S(1)} %get-tuple-element.7), channel_id=1, source_target_pairs={{1,0},{2,1},{3,2},{4,3},{5,4},{6,5},{7,6},{8,7},{9,8},{10,9},{11,1... | collective-permute-start | bytes 49160 | tf_op jit(solution)/shard_map/ppermute | solution.py:18
  124.7 3.1 %collective-permute-start.2 = (bf16[2,16,2,128]{3,2,1,0:T(2,128)(2,1)S(1)}, bf16[2,16,2,128]{3,2,1,0:T(2,128)(2,1)S(1)}, u32[]{:S(2)}, u32[]{:S(2)}) collective-permute-start(bf16[2,16,2,128]{3,2,1,0:T(2,128)(2,1)S(1)} %get-tuple-element.8), channel_id=1, source_target_pairs={{0,1},{1,2},{2,3},{3,4},{4,5},{5,6},{6,7},{7,8},{8,9},{9,10},{10,1... | collective-permute-start | bytes 49160 | tf_op jit(solution)/shard_map/ppermute | solution.py:15
Sparse Core Ops, SparseCore 0:
  135.3 106.0 reduce-scatter.1
where the time goes:
time: 249 us; the launch traced here: 248 us
  waiting for transfers between devices  161 us (65%)
  starting transfers between devices  28.2 us (11%)
  matrix products  23.6 us (9%)
  between operations  16.1 us (6%)
  local copies, waits for them, and re-layouts  15.8 us (6%)
  other arithmetic  3.77 us (2%)
    reduce_scatter x1, waiting for transfers between devices, on_device(): lax.psum_scatter(term.reshape(own_bases * lax.axis_size('date'), 2, rows,...  106 us
    all_to_all x1, waiting for transfers between devices, on_device(): lax.all_to_all(grouped, 'date', split_axis=2, concat_axis=1, tiled=True)  27.7 us
    all_to_all x1, waiting for transfers between devices, on_device(): lax.all_to_all(wiener[:, :, None, :], 'date', split_axis=1, concat_axis=2...  25.9 us
    ppermute x2, starting transfers between devices, padded_2(): lax.ppermute(lax.slice_in_dim(block, 0, width, axis=dim), axis, backward)  13.1 us
    all_to_all x1, starting transfers between devices, on_device(): lax.all_to_all(grouped, 'date', split_axis=2, concat_axis=1, tiled=True)  6.9 us
    dot_general x13, matrix products, complex_product(): jnp.dot(left_re, right_re, precision=highest)  5.31 us
    dot_general x13, matrix products, complex_product(): jnp.dot(left_re, right_im, precision=highest)  5.05 us
  transfers between devices with their start and end apart: 7, of which 4 were waited for; matrix products, arithmetic and copies ran while one was open for 1% of the time, Pallas kernels for 0%

commit v1 on v0

v1 whole, which is shorter than its diff:
```python
import functools

import jax
import jax.numpy as jnp
from jax import lax
from jax.experimental import pallas as pl
from jax.experimental.pallas import tpu as pltpu
from jax.sharding import PartitionSpec as P

NS_ITERS = 6
REACH = 2
INTERPRET = False


def filter_kernel(slc_ref, low_ref, high_ref, taps_ref, out_ref, held):
    _, dates, rows, cols = slc_ref.shape
    blocks = out_ref.shape[0]
    block_rows = rows // blocks
    pitch = held.shape[0] // dates
    taps = [
        jnp.broadcast_to(taps_ref[:, j : j + 1], (dates, cols)) for j in range(2 * REACH + 1)
    ]
    for c in range(2):
        for t in range(dates):
            held[pl.ds(t * pitch, rows), :] = slc_ref[c, t].astype(jnp.float32)

        def line(r):
            if r < 0:
                return low_ref[c, r + REACH].astype(jnp.float32)
            if r >= rows:
                return high_ref[c, r - rows].astype(jnp.float32)
            return held[pl.ds(r, dates, stride=pitch), :]

        window = [line(r) for r in range(-REACH, REACH)]
        for r in range(rows):
            window.append(line(r + REACH))
            total = taps[0] * window[0]
            for j in range(1, 2 * REACH + 1):
                total = total + taps[j] * window[j]
            window.pop(0)
            b, i = divmod(r, block_rows)
            out_ref[b, c, :, i * cols : (i + 1) * cols] = total.astype(jnp.bfloat16)


def split(x):
    hi = x.astype(jnp.bfloat16)
    return hi, (x - hi.astype(jnp.float32)).astype(jnp.bfloat16)


def dot(a, b):
    return jnp.dot(a, b, preferred_element_type=jnp.float32)


def dot3(a, b):
    a_hi, a_lo = split(a)
    b_hi, b_lo = split(b)
    return dot(
        jnp.concatenate([a_hi, a_lo, a_hi], 1), jnp.concatenate([b_hi, b_hi, b_lo], 0)
    )


def total(x):
    return jnp.sum(jnp.sum(x, axis=1, keepdims=True), axis=0, keepdims=True)


def link_kernel(pix_ref, look_ref, level_ref, half_ref, basis_ref, out_ref, stage):
    groups, _, dates_own, pixels = pix_ref.shape
    dates = groups * dates_own
    looks = look_ref.shape[1] // 2
    cols = stage.shape[2]
    block_rows = pixels // cols
    z = jnp.concatenate(
        [pix_ref[:, c].reshape(dates, pixels) for c in range(2)], axis=0
    )
    place = lax.broadcasted_iota(jnp.int32, (pixels, 2 * looks), 0)
    picked = (place == look_ref[...]).astype(jnp.float32).astype(jnp.bfloat16)
    samples = dot(z, picked)
    first = lax.broadcasted_iota(jnp.int32, (dates, 2 * looks), 1) < looks
    samp_re = samples[:dates]
    samp_im = samples[dates:]
    tall = jnp.concatenate(
        [jnp.where(first, samp_re, -samp_im), jnp.where(first, samp_im, samp_re)], 0
    )
    wide = tall.T.astype(jnp.bfloat16)
    tall = tall.astype(jnp.bfloat16)
    inner = dot(wide, tall)

    width = 2 * looks
    rows_i = lax.broadcasted_iota(jnp.int32, (width, width), 0)
    cols_i = lax.broadcasted_iota(jnp.int32, (width, width), 1)
    identity = (rows_i == cols_i).astype(jnp.float32)
    trace = total(inner * identity) * 0.5
    square = total(inner * inner) * 0.5
    mean = trace / (looks * dates) + 1e-06
    weight = level_ref[...].astype(jnp.float32) / 16.0
    alpha = weight * mean + mean
    beta = (1.0 - weight) / looks
    scale = 1.0 / jnp.sqrt(
        dates * alpha * alpha + 2.0 * alpha * beta * trace + beta * beta * square
    )

    t = scale * alpha
    x = jnp.ones_like(t)
    w = (scale * beta) * inner
    m = (2.0 - 2.0 * t) * identity - w
    u = -identity
    w = (2.0 - 2.0 * t) * w - dot3(w, w)
    x, t = x * (2.0 - t), 2.0 * t - t * t
    for step in range(1, NS_ITERS):
        last = step == NS_ITERS - 1
        stack = [m, u] if last else [m, u, w]
        prod = dot3(jnp.concatenate(stack, 0), w)
        m, u = (
            (2.0 - 2.0 * t) * m - prod[:width],
            (2.0 - t) * u - x * m - prod[width : 2 * width],
        )
        if not last:
            w = (2.0 - 2.0 * t) * w - prod[2 * width :]
        x, t = x * (2.0 - t), 2.0 * t - t * t

    half = half_ref[...]
    share = basis_ref[...].astype(jnp.float32) / (2 * half + 1).astype(jnp.float32)
    near = jnp.concatenate(
        [jnp.where(half >= j, share, 0.0) for j in range(REACH + 1)], axis=0
    )
    near_hi, near_lo = split(near)
    seen = [
        dot(near_hi, tall[c * dates : (c + 1) * dates])
        + dot(near_lo, tall[c * dates : (c + 1) * dates])
        for c in range(2)
    ]
    core = dot3(jnp.concatenate(seen, 0), (scale * beta) * (m - (mean * scale) * u))
    plain = (t - mean * scale * x) * near
    nothing = jnp.zeros_like(plain)
    core_hi, core_lo = split(core)
    gain = (
        dot(core_hi, wide)
        + dot(core_lo, wide)
        + jnp.concatenate(
            [
                jnp.concatenate([plain, nothing], 1),
                jnp.concatenate([nothing, plain], 1),
            ],
            0,
        )
    )
    proj = dot(gain.astype(jnp.bfloat16), z)

    bases = basis_ref.shape[0]
    taps = 2 * bases * (REACH + 1) // 2

    def part(c, j, row):
        start = c * taps + abs(j) * bases
        return proj[start : start + bases, row * cols : (row + 1) * cols]

    def smoothed(c, row):
        out = None
        for j in range(-REACH, REACH + 1):
            if 0 <= row + j < block_rows:
                term = part(c, j, row + j)
                out = term if out is None else out + term
        return out

    below = [block_rows, block_rows + 1]
    above = [-2, -1]
    slots = [(0, r) for r in range(block_rows)] + [(1, r) for r in range(block_rows)]
    slots += [(0, r) for r in below] + [(1, r) for r in below]
    slots += [(1, r) for r in above] + [(0, r) for r in above]
    for q, (c, row) in enumerate(slots):
        stage[q] = smoothed(c, row)
    flat = stage.reshape(len(slots) * bases, cols)
    own = bases // groups
    for d in range(groups):
        lines = [
            [
                flat[pl.ds(q * block_rows * bases + d * own + k, block_rows, stride=bases), :]
                for q in range(3)
            ]
            for k in range(own)
        ]
        rows = [v for k in range(own) for v in lines[k][:2]] + [lines[k][2] for k in range(own)]
        out_ref[d] = jnp.concatenate(rows, 0).astype(jnp.bfloat16)


def join_kernel(part_ref, low_ref, high_ref, out_ref):
    groups = part_ref.shape[0]
    own, _, rows, cols = out_ref.shape
    block_rows = rows // groups
    sub = lax.broadcasted_iota(jnp.int32, (block_rows, cols), 0)

    def lent(ref_value, k):
        start = k * block_rows
        return ref_value[start : start + block_rows].astype(jnp.float32)

    base = own * 2 * block_rows
    for k in range(own):
        lends = (
            [lent(low_ref[...], k)]
            + [lent(part_ref[b, base:, :], k) for b in range(groups)]
            + [lent(high_ref[...], k)]
        )
        for b in range(groups):
            for c in range(2):
                start = (k * 2 + c) * block_rows
                main = part_ref[b, start : start + block_rows, :].astype(jnp.float32)
                before = lends[b]
                after = lends[b + 2]
                if c == 1:
                    before = pltpu.roll(before, block_rows - 2, 0)
                    after = pltpu.roll(after, 2, 0)
                out_ref[k, c, b * block_rows : (b + 1) * block_rows, :] = (
                    main
                    + jnp.where(sub < 2, before, 0.0)
                    + jnp.where(sub >= block_rows - 2, after, 0.0)
                )


def vmem(count):
    return [pl.BlockSpec(memory_space=pltpu.VMEM)] * count


def shifts(axis):
    count = lax.axis_size(axis)
    forward = [(i, i + 1) for i in range(count - 1)]
    return forward, [(b, a) for a, b in forward]


def on_device(slc_stack, fir_taps, look_index, shrink_level, window_half, basis):
    date_local, rows, cols = slc_stack.shape[1:]
    groups = lax.axis_size("date")
    block_rows = rows // groups
    pixels = block_rows * cols
    bases, dates = basis.shape
    own = bases // groups
    forward, backward = shifts("az")

    edge_low = jnp.swapaxes(slc_stack[:, :, rows - REACH :, :], 1, 2)
    edge_high = jnp.swapaxes(slc_stack[:, :, :REACH, :], 1, 2)
    low = lax.ppermute(edge_low, "az", forward)
    high = lax.ppermute(edge_high, "az", backward)
    pitch = rows + 8
    blocks = pl.pallas_call(
        filter_kernel,
        out_shape=jax.ShapeDtypeStruct((groups, 2, date_local, pixels), jnp.bfloat16),
        in_specs=vmem(4),
        out_specs=vmem(1)[0],
        scratch_shapes=[pltpu.VMEM((date_local * pitch, cols), jnp.float32)],
        interpret=INTERPRET,
        name="azimuth_filter",
    )(slc_stack, low, high, fir_taps)
    pix = lax.all_to_all(blocks, "date", split_axis=0, concat_axis=0, tiled=True)

    look = look_index.reshape(1, -1)
    slots = 3 * block_rows
    height = 3 * own * block_rows
    lent = pl.pallas_call(
        link_kernel,
        out_shape=jax.ShapeDtypeStruct((groups, height, cols), jnp.bfloat16),
        in_specs=vmem(5),
        out_specs=vmem(1)[0],
        scratch_shapes=[pltpu.VMEM((slots, bases, cols), jnp.float32)],
        interpret=INTERPRET,
        name="phase_link",
    )(
        pix,
        jnp.concatenate([look, look], 1),
        shrink_level,
        window_half.reshape(1, dates),
        basis,
    )
    parts = lax.all_to_all(lent, "date", split_axis=0, concat_axis=0, tiled=True)

    base = 2 * own * block_rows
    above = lax.ppermute(parts[0, base:, :], "az", backward)
    below = lax.ppermute(parts[groups - 1, base:, :], "az", forward)
    return pl.pallas_call(
        join_kernel,
        out_shape=jax.ShapeDtypeStruct((own, 2, rows, cols), jnp.float32),
        in_specs=vmem(3),
        out_specs=vmem(1)[0],
        interpret=INTERPRET,
        name="overlap_add",
    )(parts, below, above)


def solution(mesh):
    in_specs = (
        P(None, "date", "az", None),
        P("date", None),
        P("az", "date", None),
        P("az", "date"),
        P(),
        P(),
    )
    out_specs = P("date", None, "az", None)
    return jax.shard_map(
        on_device, mesh=mesh, in_specs=in_specs, out_specs=out_specs, check_vma=False
    )
```

time: 249 us -> 90.4 us (0.36)
  the two profiles are of different devices: /device:TPU:1 before, /device:TPU:23 now
where the time goes in v1:
time: 90.4 us; the launch traced here: 89.9 us
  waiting for transfers between devices  34.3 us (38%)
  starting transfers between devices  25.3 us (28%)
  blocking collectives  14.2 us (16%)
  Pallas kernels  10.2 us (11%)
  local copies, waits for them, and re-layouts  4.42 us (5%)
    all_to_all x1, waiting for transfers between devices, on_device(): lax.all_to_all(blocks, 'date', split_axis=0, concat_axis=0, tiled=True)  20.5 us
    all_to_all x1, blocking collectives, on_device(): lax.all_to_all(lent, 'date', split_axis=0, concat_axis=0, tiled=True)  14.2 us
    all_to_all x1, starting transfers between devices, on_device(): lax.all_to_all(blocks, 'date', split_axis=0, concat_axis=0, tiled=True)  10.3 us
    ppermute x1, waiting for transfers between devices, on_device(): above = lax.ppermute(parts[0, base:, :], 'az', backward)  7.2 us
    ppermute x1, waiting for transfers between devices, on_device(): high = lax.ppermute(edge_high, 'az', backward)  6.67 us
    ppermute x1, starting transfers between devices, on_device(): low = lax.ppermute(edge_low, 'az', forward)  5.9 us
    pallas_call x1, Pallas kernels, on_device(): pl.pallas_call(link_kernel, out_shape=jax.ShapeDtypeStruct((groups, heigh...  5.41 us
    ppermute x1, starting transfers between devices, on_device(): below = lax.ppermute(parts[groups - 1, base:, :], 'az', forward)  5.24 us
  transfers between devices with their start and end apart: 5, of which 3 were waited for; matrix products, arithmetic and copies ran while one was open for 1% of the time, Pallas kernels for 0%

profile of v1, /device:TPU:23, one launch (start us, length us, event | category | flops | bytes accessed | tf_op | source)
XLA Modules:
  0.0 89.9 jit_solution(8887995292180411885)
XLA Ops:
  0.0 0.9 %fusion = (bf16[2,16,2,128]{3,2,1,0:T(2,128)(2,1)S(1)}, bf16[2,16,2,128]{3,2,1,0:T(2,128)(2,1)S(1)}) fusion(bf16[2,16,128,128]{3,2,1,0:T(8,128)(2,1)} %slc_ref.1), kind=kLoop, calls=%fused_computation.5 | loop fusion | bytes 65536 | tf_op jit(solution)/shard_map/slice | solution.py:238
  0.9 5.9 %collective-permute-start = (bf16[2,2,16,128]{3,2,1,0:T(8,128)(2,1)S(1)}, bf16[2,2,16,128]{3,2,1,0:T(8,128)(2,1)S(1)}, u32[]{:S(2)}, u32[]{:S(2)}) collective-permute-start(bf16[2,2,16,128]{3,2,1,0:T(8,128)(2,1)S(1)} %bitcast.12), channel_id=1, source_target_pairs={{0,1},{1,2},{2,3},{3,4},{4,5},{5,6},{6,7},{7,8},{8,9},{9,10},{10,1... | collective-permute-start | bytes 49160 | tf_op jit(solution)/shard_map/ppermute | solution.py:239
  6.8 0.0 copy-start.6
  6.9 1.9 %collective-permute-start.1 = (bf16[2,2,16,128]{3,2,1,0:T(8,128)(2,1)S(1)}, bf16[2,2,16,128]{3,2,1,0:T(8,128)(2,1)S(1)}, u32[]{:S(2)}, u32[]{:S(2)}) collective-permute-start(bf16[2,2,16,128]{3,2,1,0:T(8,128)(2,1)S(1)} %bitcast.13), channel_id=1, source_target_pairs={{1,0},{2,1},{3,2},{4,3},{5,4},{6,5},{7,6},{8,7},{9,8},{10,9},{11,1... | collective-permute-start | bytes 49160 | tf_op jit(solution)/shard_map/ppermute | solution.py:240
  8.8 0.0 copy-done.6
  8.8 0.7 copy.9.taps_ref
  9.5 0.0 collective-permute-done.low_ref
  9.5 6.7 %collective-permute-done.1.high_ref = bf16[2,2,16,128]{3,2,1,0:T(8,128)(2,1)S(1)} collective-permute-done((bf16[2,2,16,128]{3,2,1,0:T(8,128)(2,1)S(1)}, bf16[2,2,16,128]{3,2,1,0:T(8,128)(2,1)S(1)}, u32[]{:S(2)}, u32[]{:S(2)}) %collective-permute-start.1) | collective-permute-done | bytes 16416 | tf_op jit(solution)/shard_map/ppermute | solution.py:240
  16.1 0.6 copy-done.3
  16.7 3.1 %azimuth_filter.1 = bf16[16,2,16,1024]{3,2,1,0:T(8,128)(2,1)} custom-call(bf16[2,16,128,128]{3,2,1,0:T(8,128)(2,1)} %slc_ref.1, bf16[2,2,16,128]{3,2,1,0:T(8,128)(2,1)} %copy-done.2, bf16[2,2,16,128]{3,2,1,0:T(8,128)(2,1)} %copy-done.3, f32[16,5]{1,0:T(8,128)} %copy.9.taps_ref), custom_call_target="tpu_custom_call" | custom-call | tf_op jit(solution)/shard_map/azimuth_filter/pallas_call | solution.py:242
  19.9 10.3 %all-to-all-start = ((bf16[16,2,16,1024]{3,2,1,0:T(8,128)(2,1)}), bf16[16,2,16,1024]{3,2,1,0:T(8,128)(2,1)S(1)}, u32[]{:S(2)}, u32[]{:S(2)}) async-start(bf16[16,2,16,1024]{3,2,1,0:T(8,128)(2,1)} %azimuth_filter.1), calls=%async_computation | async-start | bytes 2097152 | tf_op jit(solution)/shard_map/all_to_all | solution.py:251
  30.8 0.0 copy-start.7
  30.9 0.6 copy-done.7
  31.5 0.6 pad_add_fusion.look_ref
  32.1 20.5 %all-to-all-done.pix_ref = bf16[16,2,16,1024]{3,2,1,0:T(8,128)(2,1)S(1)} async-done(((bf16[16,2,16,1024]{3,2,1,0:T(8,128)(2,1)}), bf16[16,2,16,1024]{3,2,1,0:T(8,128)(2,1)S(1)}, u32[]{:S(2)}, u32[]{:S(2)}) %all-to-all-start) | async-done | bytes 1048608 | tf_op jit(solution)/shard_map/all_to_all | solution.py:251
  52.6 1.0 %copy-done = bf16[16,2,16,1024]{3,2,1,0:T(8,128)(2,1)} copy-done((bf16[16,2,16,1024]{3,2,1,0:T(8,128)(2,1)}, bf16[16,2,16,1024]{3,2,1,0:T(8,128)(2,1)S(1)}, u32[]{:S(2)}) %copy-start) | copy-done | bytes 1048600
  53.6 5.4 %phase_link.1 = bf16[16,48,128]{2,1,0:T(8,128)(2,1)} custom-call(bf16[16,2,16,1024]{3,2,1,0:T(8,128)(2,1)} %copy-done, s32[1,128]{1,0:T(1,128)} %pad_add_fusion.look_ref, s32[1,1]{1,0:T(1,128)S(6)} %copy.16.level_ref, s32[1,256]{1,0:T(1,128)} %bitcast.14, bf16[32,256]{1,0:T(8,128)(2,1)} %basis_ref.1), custom_call_target="tpu_custom_call" | custom-call | tf_op jit(solution)/shard_map/phase_link/pallas_call | solution.py:256
  59.0 14.2 %all_to_all.10.part_ref = bf16[16,48,128]{2,1,0:T(8,128)(2,1)S(1)} all-to-all(bf16[16,48,128]{2,1,0:T(8,128)(2,1)} %phase_link.1), channel_id=1, replica_groups=mesh['date'=16,'az'=32] {'date'}, dimensions={0} | all-to-all | bytes 393216 | tf_op jit(solution)/shard_map/all_to_all | solution.py:271
  73.2 5.2 %collective-permute-start.2 = (bf16[16,128]{1,0:T(8,128)(2,1)S(1)}, bf16[16,128]{1,0:T(8,128)(2,1)S(1)}, u32[]{:S(2)}, u32[]{:S(2)}) collective-permute-start(bf16[16,128]{1,0:T(8,128)(2,1)S(1)} %get-tuple-element.8), channel_id=1, source_target_pairs={{0,1},{1,2},{2,3},{3,4},{4,5},{5,6},{6,7},{7,8},{8,9},{9,10},{10,1... | collective-permute-start | bytes 12296 | tf_op jit(solution)/shard_map/ppermute | solution.py:275
  78.5 1.9 %collective-permute-start.3 = (bf16[16,128]{1,0:T(8,128)(2,1)S(1)}, bf16[16,128]{1,0:T(8,128)(2,1)S(1)}, u32[]{:S(2)}, u32[]{:S(2)}) collective-permute-start(bf16[16,128]{1,0:T(8,128)(2,1)S(1)} %get-tuple-element.7), channel_id=1, source_target_pairs={{1,0},{2,1},{3,2},{4,3},{5,4},{6,5},{7,6},{8,7},{9,8},{10,9},{11,1... | collective-permute-start | bytes 12296 | tf_op jit(solution)/shard_map/ppermute | solution.py:274
  80.4 0.0 collective-permute-done.2.low_ref
  80.4 7.2 %collective-permute-done.3.high_ref = bf16[16,128]{1,0:T(8,128)(2,1)S(1)} collective-permute-done((bf16[16,128]{1,0:T(8,128)(2,1)S(1)}, bf16[16,128]{1,0:T(8,128)(2,1)S(1)}, u32[]{:S(2)}, u32[]{:S(2)}) %collective-permute-start.3) | collective-permute-done | bytes 4128 | tf_op jit(solution)/shard_map/ppermute | solution.py:274
  87.6 0.6 copy-done.5
  88.2 1.7 %overlap_add.1 = f32[2,2,128,128]{3,2,1,0:T(8,128)} custom-call(bf16[16,48,128]{2,1,0:T(8,128)(2,1)} %copy-done.1, bf16[16,128]{1,0:T(8,128)(2,1)} %copy-done.4, bf16[16,128]{1,0:T(8,128)(2,1)} %copy-done.5), custom_call_target="tpu_custom_call" | custom-call | tf_op jit(solution)/shard_map/overlap_add/pallas_call | solution.py:276
  (12 shorter events, 0.0 us)
Async XLA Ops:
  0.9 8.6 %collective-permute-start = (bf16[2,2,16,128]{3,2,1,0:T(8,128)(2,1)S(1)}, bf16[2,2,16,128]{3,2,1,0:T(8,128)(2,1)S(1)}, u32[]{:S(2)}, u32[]{:S(2)}) collective-permute-start(bf16[2,2,16,128]{3,2,1,0:T(8,128)(2,1)S(1)} %bitcast.12), channel_id=1, source_target_pairs={{0,1},{1,2},{2,3},{3,4},{4,5},{5,6},{6,7},{7,8},{8,9},{9,10},{10,1... | collective-permute-start | bytes 49160 | tf_op jit(solution)/shard_map/ppermute | solution.py:239
  6.8 2.0 %copy-start.6 = (f32[16,5]{0,1:T(8,128)S(1)}, f32[16,5]{0,1:T(8,128)}, u32[]{:S(2)}) copy-start(f32[16,5]{0,1:T(8,128)} %param.7) | copy-start | bytes 964
  6.9 9.3 %collective-permute-start.1 = (bf16[2,2,16,128]{3,2,1,0:T(8,128)(2,1)S(1)}, bf16[2,2,16,128]{3,2,1,0:T(8,128)(2,1)S(1)}, u32[]{:S(2)}, u32[]{:S(2)}) collective-permute-start(bf16[2,2,16,128]{3,2,1,0:T(8,128)(2,1)S(1)} %bitcast.13), channel_id=1, source_target_pairs={{1,0},{2,1},{3,2},{4,3},{5,4},{6,5},{7,6},{8,7},{9,8},{10,9},{11,1... | collective-permute-start | bytes 49160 | tf_op jit(solution)/shard_map/ppermute | solution.py:240
  9.5 6.7 %copy-start.2 = (bf16[2,2,16,128]{3,2,1,0:T(8,128)(2,1)}, bf16[2,2,16,128]{3,2,1,0:T(8,128)(2,1)S(1)}, u32[]{:S(2)}) copy-start(bf16[2,2,16,128]{3,2,1,0:T(8,128)(2,1)S(1)} %collective-permute-done.low_ref) | copy-start | bytes 49156
  16.1 0.6 copy-start.3
  19.9 32.7 %all-to-all-start = ((bf16[16,2,16,1024]{3,2,1,0:T(8,128)(2,1)}), bf16[16,2,16,1024]{3,2,1,0:T(8,128)(2,1)S(1)}, u32[]{:S(2)}, u32[]{:S(2)}) async-start(bf16[16,2,16,1024]{3,2,1,0:T(8,128)(2,1)} %azimuth_filter.1), calls=%async_computation | async-start | bytes 2097152 | tf_op jit(solution)/shard_map/all_to_all | solution.py:251
  30.8 0.7 copy-start.7
  52.6 1.0 %copy-start = (bf16[16,2,16,1024]{3,2,1,0:T(8,128)(2,1)}, bf16[16,2,16,1024]{3,2,1,0:T(8,128)(2,1)S(1)}, u32[]{:S(2)}) copy-start(bf16[16,2,16,1024]{3,2,1,0:T(8,128)(2,1)S(1)} %all-to-all-done.pix_ref) | copy-start | bytes 3145732
  73.2 14.4 %copy-start.1 = (bf16[16,48,128]{2,1,0:T(8,128)(2,1)}, bf16[16,48,128]{2,1,0:T(8,128)(2,1)S(1)}, u32[]{:S(2)}) copy-start(bf16[16,48,128]{2,1,0:T(8,128)(2,1)S(1)} %all_to_all.10.part_ref) | copy-start | bytes 589828
  73.2 7.2 %collective-permute-start.2 = (bf16[16,128]{1,0:T(8,128)(2,1)S(1)}, bf16[16,128]{1,0:T(8,128)(2,1)S(1)}, u32[]{:S(2)}, u32[]{:S(2)}) collective-permute-start(bf16[16,128]{1,0:T(8,128)(2,1)S(1)} %get-tuple-element.8), channel_id=1, source_target_pairs={{0,1},{1,2},{2,3},{3,4},{4,5},{5,6},{6,7},{7,8},{8,9},{9,10},{10,1... | collective-permute-start | bytes 12296 | tf_op jit(solution)/shard_map/ppermute | solution.py:275
  78.5 9.1 %collective-permute-start.3 = (bf16[16,128]{1,0:T(8,128)(2,1)S(1)}, bf16[16,128]{1,0:T(8,128)(2,1)S(1)}, u32[]{:S(2)}, u32[]{:S(2)}) collective-permute-start(bf16[16,128]{1,0:T(8,128)(2,1)S(1)} %get-tuple-element.7), channel_id=1, source_target_pairs={{1,0},{2,1},{3,2},{4,3},{5,4},{6,5},{7,6},{8,7},{9,8},{10,9},{11,1... | collective-permute-start | bytes 12296 | tf_op jit(solution)/shard_map/ppermute | solution.py:274
  80.4 7.2 %copy-start.4 = (bf16[16,128]{1,0:T(8,128)(2,1)}, bf16[16,128]{1,0:T(8,128)(2,1)S(1)}, u32[]{:S(2)}) copy-start(bf16[16,128]{1,0:T(8,128)(2,1)S(1)} %collective-permute-done.2.low_ref) | copy-start | bytes 12292
  87.6 0.6 copy-start.5

commit v2 on v1

--- a/solution.py
+++ b/solution.py
@@ -215,6 +215,14 @@
                 )
 
 
+def on_chip(x):
+    return pltpu.with_memory_space_constraint(x, pltpu.VMEM) if not INTERPRET else x
+
+
+def chip_out(shape, dtype):
+    return jax.ShapeDtypeStruct(shape, dtype) if INTERPRET else pltpu.VMEM(shape, dtype)
+
+
 def vmem(count):
     return [pl.BlockSpec(memory_space=pltpu.VMEM)] * count
 
@@ -241,13 +249,13 @@
     pitch = rows + 8
     blocks = pl.pallas_call(
         filter_kernel,
-        out_shape=jax.ShapeDtypeStruct((groups, 2, date_local, pixels), jnp.bfloat16),
+        out_shape=chip_out((groups, 2, date_local, pixels), jnp.bfloat16),
         in_specs=vmem(4),
         out_specs=vmem(1)[0],
         scratch_shapes=[pltpu.VMEM((date_local * pitch, cols), jnp.float32)],
         interpret=INTERPRET,
         name="azimuth_filter",
-    )(slc_stack, low, high, fir_taps)
+    )(slc_stack, on_chip(low), on_chip(high), fir_taps)
     pix = lax.all_to_all(blocks, "date", split_axis=0, concat_axis=0, tiled=True)
 
     look = look_index.reshape(1, -1)
@@ -255,14 +263,14 @@
     height = 3 * own * block_rows
     lent = pl.pallas_call(
         link_kernel,
-        out_shape=jax.ShapeDtypeStruct((groups, height, cols), jnp.bfloat16),
+        out_shape=chip_out((groups, height, cols), jnp.bfloat16),
         in_specs=vmem(5),
         out_specs=vmem(1)[0],
         scratch_shapes=[pltpu.VMEM((slots, bases, cols), jnp.float32)],
         interpret=INTERPRET,
         name="phase_link",
     )(
-        pix,
+        on_chip(pix),
         jnp.concatenate([look, look], 1),
         shrink_level,
         window_half.reshape(1, dates),
@@ -280,7 +288,7 @@
         out_specs=vmem(1)[0],
         interpret=INTERPRET,
         name="overlap_add",
-    )(parts, below, above)
+    )(on_chip(parts), on_chip(below), on_chip(above))
 
 
 def solution(mesh):

time: 90.4 us -> 85.9 us (0.950)
  local copies, waits for them, and re-layouts: 4.42 us -> 2.25 us
  Pallas kernels: 10.2 us -> 8.12 us
    unnamed x19 -> x7, local copies, waits for them, and re-layouts: 3.52 us -> 1.35 us
    pallas_call x2, Pallas kernels: 8.56 us -> 7.36 us  [the longest x1 4.25 us: on_device(): pl.pallas_call(link_kernel, out_shape=chip_out((groups, height, cols), jn...]
    pallas_call x1, Pallas kernels: 1.69 us -> 0.76 us  [on_device(): pl.pallas_call(join_kernel, out_shape=jax.ShapeDtypeStruct((own, 2, rows,...]
where the time goes in v2:
time: 85.9 us; the launch traced here: 85.4 us
  waiting for transfers between devices  34.4 us (40%)
  starting transfers between devices  25.3 us (29%)
  blocking collectives  14 us (16%)
  Pallas kernels  8.12 us (9%)
  local copies, waits for them, and re-layouts  2.25 us (3%)
    all_to_all x1, waiting for transfers between devices, on_device(): lax.all_to_all(blocks, 'date', split_axis=0, concat_axis=0, tiled=True)  20.5 us
    all_to_all x1, blocking collectives, on_device(): lax.all_to_all(lent, 'date', split_axis=0, concat_axis=0, tiled=True)  14 us
    all_to_all x1, starting transfers between devices, on_device(): lax.all_to_all(blocks, 'date', split_axis=0, concat_axis=0, tiled=True)  10.3 us
    ppermute x1, waiting for transfers between devices, on_device(): above = lax.ppermute(parts[0, base:, :], 'az', backward)  7.21 us
    ppermute x1, waiting for transfers between devices, on_device(): high = lax.ppermute(edge_high, 'az', backward)  6.66 us
    ppermute x1, starting transfers between devices, on_device(): low = lax.ppermute(edge_low, 'az', forward)  5.9 us
    ppermute x1, starting transfers between devices, on_device(): below = lax.ppermute(parts[groups - 1, base:, :], 'az', forward)  5.23 us
    pallas_call x1, Pallas kernels, on_device(): pl.pallas_call(link_kernel, out_shape=chip_out((groups, height, cols), jn...  4.25 us
  transfers between devices with their start and end apart: 5, of which 3 were waited for; matrix products, arithmetic and copies ran while one was open for 1% of the time, Pallas kernels for 0%

profile of v2, /device:TPU:23, one launch (start us, length us, event | category | flops | bytes accessed | tf_op | source)
XLA Modules:
  0.0 85.4 jit_solution(18188545597547453322)
XLA Ops:
  0.0 0.9 %fusion = (bf16[2,16,2,128]{3,2,1,0:T(2,128)(2,1)S(1)}, bf16[2,16,2,128]{3,2,1,0:T(2,128)(2,1)S(1)}) fusion(bf16[2,16,128,128]{3,2,1,0:T(8,128)(2,1)} %slc_ref.1), kind=kLoop, calls=%fused_computation.5 | loop fusion | bytes 65536 | tf_op jit(solution)/shard_map/slice | solution.py:246
  0.9 5.9 %collective-permute-start = (bf16[2,2,16,128]{3,2,1,0:T(8,128)(2,1)S(1)}, bf16[2,2,16,128]{3,2,1,0:T(8,128)(2,1)S(1)}, u32[]{:S(2)}, u32[]{:S(2)}) collective-permute-start(bf16[2,2,16,128]{3,2,1,0:T(8,128)(2,1)S(1)} %bitcast.12), channel_id=1, source_target_pairs={{0,1},{1,2},{2,3},{3,4},{4,5},{5,6},{6,7},{7,8},{8,9},{9,10},{10,1... | collective-permute-start | bytes 49160 | tf_op jit(solution)/shard_map/ppermute | solution.py:247
  6.8 0.0 copy-start
  6.9 1.9 %collective-permute-start.1 = (bf16[2,2,16,128]{3,2,1,0:T(8,128)(2,1)S(1)}, bf16[2,2,16,128]{3,2,1,0:T(8,128)(2,1)S(1)}, u32[]{:S(2)}, u32[]{:S(2)}) collective-permute-start(bf16[2,2,16,128]{3,2,1,0:T(8,128)(2,1)S(1)} %bitcast.13), channel_id=1, source_target_pairs={{1,0},{2,1},{3,2},{4,3},{5,4},{6,5},{7,6},{8,7},{9,8},{10,9},{11,1... | collective-permute-start | bytes 49160 | tf_op jit(solution)/shard_map/ppermute | solution.py:248
  8.8 0.0 copy-done
  8.8 0.7 copy.9.taps_ref
  9.5 0.0 collective-permute-done.low_ref
  9.5 6.7 %collective-permute-done.1.high_ref = bf16[2,2,16,128]{3,2,1,0:T(8,128)(2,1)S(1)} collective-permute-done((bf16[2,2,16,128]{3,2,1,0:T(8,128)(2,1)S(1)}, bf16[2,2,16,128]{3,2,1,0:T(8,128)(2,1)S(1)}, u32[]{:S(2)}, u32[]{:S(2)}) %collective-permute-start.1) | collective-permute-done | bytes 16416 | tf_op jit(solution)/shard_map/ppermute | solution.py:248
  16.1 3.1 %azimuth_filter.1 = bf16[16,2,16,1024]{3,2,1,0:T(8,128)(2,1)} custom-call(bf16[2,16,128,128]{3,2,1,0:T(8,128)(2,1)} %slc_ref.1, bf16[2,2,16,128]{3,2,1,0:T(8,128)(2,1)S(1)} %collective-permute-done.low_ref, bf16[2,2,16,128]{3,2,1,0:T(8,128)(2,1)S(1)} %collective-permute-done.1.high_ref, f32[16,5]{1,0:T(8,128)} %copy.9.taps_ref), custom_call_target="tpu_custom_call" | custom-call | tf_op jit(solution)/shard_map/azimuth_filter/pallas_call | solution.py:250
  19.2 10.3 %all-to-all-start = ((bf16[16,2,16,1024]{3,2,1,0:T(8,128)(2,1)}), bf16[16,2,16,1024]{3,2,1,0:T(8,128)(2,1)S(1)}, u32[]{:S(2)}, u32[]{:S(2)}) async-start(bf16[16,2,16,1024]{3,2,1,0:T(8,128)(2,1)} %azimuth_filter.1), calls=%async_computation | async-start | bytes 2097152 | tf_op jit(solution)/shard_map/all_to_all | solution.py:259
  30.2 0.0 copy-start.1
  30.2 0.6 copy-done.1
  30.9 0.6 pad_add_fusion.look_ref
  31.5 20.5 %all-to-all-done.pix_ref = bf16[16,2,16,1024]{3,2,1,0:T(8,128)(2,1)S(1)} async-done(((bf16[16,2,16,1024]{3,2,1,0:T(8,128)(2,1)}), bf16[16,2,16,1024]{3,2,1,0:T(8,128)(2,1)S(1)}, u32[]{:S(2)}, u32[]{:S(2)}) %all-to-all-start) | async-done | bytes 1048608 | tf_op jit(solution)/shard_map/all_to_all | solution.py:259
  52.0 4.3 %phase_link.1 = bf16[16,48,128]{2,1,0:T(8,128)(2,1)S(1)} custom-call(bf16[16,2,16,1024]{3,2,1,0:T(8,128)(2,1)S(1)} %all-to-all-done.pix_ref, s32[1,128]{1,0:T(1,128)} %pad_add_fusion.look_ref, s32[1,1]{1,0:T(1,128)S(6)} %copy.16.level_ref, s32[1,256]{1,0:T(1,128)} %bitcast.14, bf16[32,256]{1,0:T(8,128)(2,1)} %basis_ref.1), custom_call_target="tpu_custom_call" | custom-call | tf_op jit(solution)/shard_map/phase_link/pallas_call | solution.py:264
  56.2 14.0 %all_to_all.10.part_ref = bf16[16,48,128]{2,1,0:T(8,128)(2,1)S(1)} all-to-all(bf16[16,48,128]{2,1,0:T(8,128)(2,1)S(1)} %phase_link.1), channel_id=1, replica_groups=mesh['date'=16,'az'=32] {'date'}, dimensions={0} | all-to-all | bytes 393216 | tf_op jit(solution)/shard_map/all_to_all | solution.py:279
  70.3 5.2 %collective-permute-start.2 = (bf16[16,128]{1,0:T(8,128)(2,1)S(1)}, bf16[16,128]{1,0:T(8,128)(2,1)S(1)}, u32[]{:S(2)}, u32[]{:S(2)}) collective-permute-start(bf16[16,128]{1,0:T(8,128)(2,1)S(1)} %get-tuple-element.8), channel_id=1, source_target_pairs={{0,1},{1,2},{2,3},{3,4},{4,5},{5,6},{6,7},{7,8},{8,9},{9,10},{10,1... | collective-permute-start | bytes 12296 | tf_op jit(solution)/shard_map/ppermute | solution.py:283
  75.5 1.9 %collective-permute-start.3 = (bf16[16,128]{1,0:T(8,128)(2,1)S(1)}, bf16[16,128]{1,0:T(8,128)(2,1)S(1)}, u32[]{:S(2)}, u32[]{:S(2)}) collective-permute-start(bf16[16,128]{1,0:T(8,128)(2,1)S(1)} %get-tuple-element.7), channel_id=1, source_target_pairs={{1,0},{2,1},{3,2},{4,3},{5,4},{6,5},{7,6},{8,7},{9,8},{10,9},{11,1... | collective-permute-start | bytes 12296 | tf_op jit(solution)/shard_map/ppermute | solution.py:282
  77.4 0.0 collective-permute-done.2.low_ref
  77.4 7.2 %collective-permute-done.3.high_ref = bf16[16,128]{1,0:T(8,128)(2,1)S(1)} collective-permute-done((bf16[16,128]{1,0:T(8,128)(2,1)S(1)}, bf16[16,128]{1,0:T(8,128)(2,1)S(1)}, u32[]{:S(2)}, u32[]{:S(2)}) %collective-permute-start.3) | collective-permute-done | bytes 4128 | tf_op jit(solution)/shard_map/ppermute | solution.py:282
  84.6 0.8 overlap_add.1
  (3 shorter events, 0.0 us)
Async XLA Ops:
  0.9 8.6 %collective-permute-start = (bf16[2,2,16,128]{3,2,1,0:T(8,128)(2,1)S(1)}, bf16[2,2,16,128]{3,2,1,0:T(8,128)(2,1)S(1)}, u32[]{:S(2)}, u32[]{:S(2)}) collective-permute-start(bf16[2,2,16,128]{3,2,1,0:T(8,128)(2,1)S(1)} %bitcast.12), channel_id=1, source_target_pairs={{0,1},{1,2},{2,3},{3,4},{4,5},{5,6},{6,7},{7,8},{8,9},{9,10},{10,1... | collective-permute-start | bytes 49160 | tf_op jit(solution)/shard_map/ppermute | solution.py:247
  6.8 2.0 %copy-start = (f32[16,5]{0,1:T(8,128)S(1)}, f32[16,5]{0,1:T(8,128)}, u32[]{:S(2)}) copy-start(f32[16,5]{0,1:T(8,128)} %param.7) | copy-start | bytes 964
  6.9 9.3 %collective-permute-start.1 = (bf16[2,2,16,128]{3,2,1,0:T(8,128)(2,1)S(1)}, bf16[2,2,16,128]{3,2,1,0:T(8,128)(2,1)S(1)}, u32[]{:S(2)}, u32[]{:S(2)}) collective-permute-start(bf16[2,2,16,128]{3,2,1,0:T(8,128)(2,1)S(1)} %bitcast.13), channel_id=1, source_target_pairs={{1,0},{2,1},{3,2},{4,3},{5,4},{6,5},{7,6},{8,7},{9,8},{10,9},{11,1... | collective-permute-start | bytes 49160 | tf_op jit(solution)/shard_map/ppermute | solution.py:248
  19.2 32.7 %all-to-all-start = ((bf16[16,2,16,1024]{3,2,1,0:T(8,128)(2,1)}), bf16[16,2,16,1024]{3,2,1,0:T(8,128)(2,1)S(1)}, u32[]{:S(2)}, u32[]{:S(2)}) async-start(bf16[16,2,16,1024]{3,2,1,0:T(8,128)(2,1)} %azimuth_filter.1), calls=%async_computation | async-start | bytes 2097152 | tf_op jit(solution)/shard_map/all_to_all | solution.py:259
  30.2 0.7 copy-start.1
  70.3 7.2 %collective-permute-start.2 = (bf16[16,128]{1,0:T(8,128)(2,1)S(1)}, bf16[16,128]{1,0:T(8,128)(2,1)S(1)}, u32[]{:S(2)}, u32[]{:S(2)}) collective-permute-start(bf16[16,128]{1,0:T(8,128)(2,1)S(1)} %get-tuple-element.8), channel_id=1, source_target_pairs={{0,1},{1,2},{2,3},{3,4},{4,5},{5,6},{6,7},{7,8},{8,9},{9,10},{10,1... | collective-permute-start | bytes 12296 | tf_op jit(solution)/shard_map/ppermute | solution.py:283
  75.5 9.1 %collective-permute-start.3 = (bf16[16,128]{1,0:T(8,128)(2,1)S(1)}, bf16[16,128]{1,0:T(8,128)(2,1)S(1)}, u32[]{:S(2)}, u32[]{:S(2)}) collective-permute-start(bf16[16,128]{1,0:T(8,128)(2,1)S(1)} %get-tuple-element.7), channel_id=1, source_target_pairs={{1,0},{2,1},{3,2},{4,3},{5,4},{6,5},{7,6},{8,7},{9,8},{10,9},{11,1... | collective-permute-start | bytes 12296 | tf_op jit(solution)/shard_map/ppermute | solution.py:282

commit v3 on v2

v3 whole, which is shorter than its diff:
```python
import jax
import jax.numpy as jnp
from jax import lax
from jax.experimental import pallas as pl
from jax.experimental.pallas import tpu as pltpu
from jax.sharding import PartitionSpec as P

NS_ITERS = 6
REACH = 2
INTERPRET = False


def filter_kernel(
    odd_ref, slc_hbm, near_ref, far_ref, taps_ref, out_ref, slc_ref, held, done, load_sems, sems
):
    _, dates, rows, cols = slc_ref.shape
    blocks = out_ref.shape[0]
    block_rows = rows // blocks
    pitch = held.shape[0] // dates
    even = odd_ref[0, 0] == 0
    taps = [
        jnp.broadcast_to(taps_ref[:, j : j + 1], (dates, cols)) for j in range(2 * REACH + 1)
    ]
    parts = sems.shape[0] // 2
    share = blocks // parts
    copies = []
    loads = [
        pltpu.make_async_copy(slc_hbm.at[c], slc_ref.at[c], load_sems.at[c]) for c in range(2)
    ]
    for load in loads:
        load.start()
    for c in range(2):
        loads[c].wait()
        for t in range(dates):
            held[pl.ds(t * pitch, rows), :] = slc_ref[c, t].astype(jnp.float32)

        def line(r):
            if r < 0:
                pick = jnp.where(even, far_ref[c, r + REACH], near_ref[c, r + REACH])
                return pick.astype(jnp.float32)
            if r >= rows:
                pick = jnp.where(even, near_ref[c, r - rows], far_ref[c, r - rows])
                return pick.astype(jnp.float32)
            return held[pl.ds(r, dates, stride=pitch), :]

        window = [line(r) for r in range(-REACH, REACH)]
        for r in range(rows):
            window.append(line(r + REACH))
            total = taps[0] * window[0]
            for j in range(1, 2 * REACH + 1):
                total = total + taps[j] * window[j]
            window.pop(0)
            b, i = divmod(r, block_rows)
            done[b, c, :, i * cols : (i + 1) * cols] = total.astype(jnp.bfloat16)
            if (r + 1) % (share * block_rows) == 0:
                part = b // share
                copy = pltpu.make_async_copy(
                    done.at[pl.ds(part * share, share), c],
                    out_ref.at[pl.ds(part * share, share), c],
                    sems.at[c * parts + part],
                )
                copy.start()
                copies.append(copy)
    for copy in copies:
        copy.wait()


def split(x):
    hi = x.astype(jnp.bfloat16)
    return hi, (x - hi.astype(jnp.float32)).astype(jnp.bfloat16)


def dot(a, b):
    return jnp.dot(a, b, preferred_element_type=jnp.float32)


def dot3(a, b):
    a_hi, a_lo = split(a)
    b_hi, b_lo = split(b)
    return dot(
        jnp.concatenate([a_hi, a_lo, a_hi], 1), jnp.concatenate([b_hi, b_hi, b_lo], 0)
    )


def total(x):
    return jnp.sum(jnp.sum(x, axis=1, keepdims=True), axis=0, keepdims=True)


def link_kernel(
    date_ref, pix_ref, look_ref, level_ref, half_ref, basis_ref, stage_ref, edge_ref, proj
):
    groups, _, dates_own, pixels = pix_ref.shape
    dates = groups * dates_own
    width = look_ref.shape[1]
    looks = width // 2
    bases = basis_ref.shape[0]
    cols = stage_ref.shape[2]
    block_rows = pixels // cols
    place = lax.broadcasted_iota(jnp.int32, (pixels, width), 0)
    picked = (place == look_ref[...]).astype(jnp.float32).astype(jnp.bfloat16)
    samp_re = dot(pix_ref[:, 0].reshape(dates, pixels), picked)
    samp_im = dot(pix_ref[:, 1].reshape(dates, pixels), picked)
    first = lax.broadcasted_iota(jnp.int32, (dates, width), 1) < looks
    tall = jnp.concatenate(
        [jnp.where(first, samp_re, -samp_im), jnp.where(first, samp_im, samp_re)], 0
    )
    wide = tall.T.astype(jnp.bfloat16)
    tall = tall.astype(jnp.bfloat16)
    inner = dot(wide[:looks], tall)

    half = half_ref[...]
    share = basis_ref[...].astype(jnp.float32) / (2 * half + 1).astype(jnp.float32)
    near = jnp.concatenate(
        [jnp.where(half >= j, share, 0.0) for j in range(REACH + 1)], axis=0
    )
    near_hi, near_lo = split(near)
    seen = dot(near_hi, tall[:dates]) + dot(near_lo, tall[:dates])

    rows_i = lax.broadcasted_iota(jnp.int32, (looks, width), 0)
    cols_i = lax.broadcasted_iota(jnp.int32, (looks, width), 1)
    identity = (rows_i == cols_i).astype(jnp.float32)
    turn = jnp.where(cols_i < looks, -1.0, 1.0)

    def whole(top):
        return jnp.concatenate([top, turn * pltpu.roll(top, looks, 1)], 0)

    trace = total(inner * identity)
    square = total(inner * inner)
    mean = trace / (looks * dates) + 1e-06
    weight = level_ref[...].astype(jnp.float32) / 16.0
    alpha = weight * mean + mean
    beta = (1.0 - weight) / looks
    scale = 1.0 / jnp.sqrt(
        dates * alpha * alpha + 2.0 * alpha * beta * trace + beta * beta * square
    )

    t = scale * alpha
    x = jnp.ones_like(t)
    w = (scale * beta) * inner
    m = (2.0 - 2.0 * t) * identity - w
    u = -identity
    w = (2.0 - 2.0 * t) * w - dot3(w, whole(w))
    x, t = x * (2.0 - t), 2.0 * t - t * t
    for step in range(1, NS_ITERS):
        full = whole(w)
        if step < NS_ITERS - 1:
            w = (2.0 - 2.0 * t) * w - dot3(w, full)
        prod = dot3(jnp.concatenate([m, u], 0), full)
        m, u = (
            (2.0 - 2.0 * t) * m - prod[:looks],
            (2.0 - t) * u - x * m - prod[looks:],
        )
        x, t = x * (2.0 - t), 2.0 * t - t * t

    core = dot3(seen, whole((scale * beta) * (m - (mean * scale) * u)))
    core_hi, core_lo = split(core)
    gain = dot(core_hi, wide) + dot(core_lo, wide)
    plain = (t - mean * scale * x) * near
    left = gain[:, :dates] + plain
    right = gain[:, dates:]
    gain_re = jnp.concatenate([left, -right], 0).astype(jnp.bfloat16)
    gain_im = jnp.concatenate([right, left], 0).astype(jnp.bfloat16)
    proj[...] = dot(gain_re, pix_ref[:, 0].reshape(dates, pixels)) + dot(
        gain_im, pix_ref[:, 1].reshape(dates, pixels)
    )

    below = [block_rows, block_rows + 1]
    above = [-2, -1]
    slots = [(0, r) for r in range(block_rows)] + [(1, r) for r in range(block_rows)]
    slots += [(0, r) for r in below] + [(1, r) for r in below]
    slots += [(1, r) for r in above] + [(0, r) for r in above]
    sub = 8
    opens = date_ref[0, 0] == 0
    for k in range(0, bases, sub):
        rest = {}
        for c in range(2):
            terms = [
                [
                    proj[
                        pl.ds((c * (REACH + 1) + j) * bases + k, sub),
                        pl.ds(row * cols, cols),
                    ]
                    for row in range(block_rows)
                ]
                for j in range(REACH + 1)
            ]
            for q, (part, row) in enumerate(slots):
                if part != c:
                    continue
                out = None
                for j in range(-REACH, REACH + 1):
                    if 0 <= row + j < block_rows:
                        term = terms[abs(j)][row + j]
                        out = term if out is None else out + term
                stage_ref[q, pl.ds(k, sub), :] = out
                rest[q] = out
        base = 2 * block_rows
        for i in range(2 * REACH):
            edge = jnp.where(opens, rest[base + 2 * REACH + i], rest[base + i])
            edge_ref[i, pl.ds(k, sub), :] = edge.astype(jnp.bfloat16)


def pack_kernel(date_ref, stage_ref, edge_ref, out_ref, held):
    groups = out_ref.shape[0]
    slots, bases, cols = stage_ref.shape
    sub = slots // 3
    own = bases // groups
    opens = date_ref[0, 0] == 0
    closes = date_ref[0, 0] == groups - 1
    for q in range(slots):
        value = stage_ref[q]
        i = q - 2 * sub
        if i >= 2 * REACH:
            value = jnp.where(opens, edge_ref[i - 2 * REACH].astype(jnp.float32), value)
        elif i >= 0:
            value = jnp.where(closes, edge_ref[i].astype(jnp.float32), value)
        held[pl.ds(q * bases, bases), :] = value
    for d in range(groups):
        lines = [
            [
                held[pl.ds(q * sub * bases + d * own + k, sub, stride=bases), :]
                for q in range(3)
            ]
            for k in range(own)
        ]
        rows = [v for k in range(own) for v in lines[k][:2]] + [lines[k][2] for k in range(own)]
        out_ref[d] = jnp.concatenate(rows, 0).astype(jnp.bfloat16)


def join_kernel(part_ref, out_ref):
    groups = part_ref.shape[0]
    own, _, rows, cols = out_ref.shape
    block_rows = rows // groups
    sub = lax.broadcasted_iota(jnp.int32, (block_rows, cols), 0)
    base = own * 2 * block_rows
    for k in range(own):
        start = base + k * block_rows
        lends = [
            part_ref[b, start : start + block_rows, :].astype(jnp.float32)
            for b in range(groups)
        ]
        for b in range(groups):
            for c in range(2):
                start = (k * 2 + c) * block_rows
                main = part_ref[b, start : start + block_rows, :].astype(jnp.float32)
                if b:
                    before = pltpu.roll(lends[b - 1], block_rows - 2, 0) if c else lends[b - 1]
                else:
                    before = pltpu.roll(lends[0], 2 if c else 4, 0)
                if b < groups - 1:
                    after = pltpu.roll(lends[b + 1], 2, 0) if c else lends[b + 1]
                else:
                    after = pltpu.roll(lends[b], block_rows - 2 if c else 4, 0)
                out_ref[k, c, b * block_rows : (b + 1) * block_rows, :] = (
                    main
                    + jnp.where(sub < 2, before, 0.0)
                    + jnp.where(sub >= block_rows - 2, after, 0.0)
                )


def on_chip(x):
    return x if INTERPRET else pltpu.with_memory_space_constraint(x, pltpu.VMEM)


def chip_out(shape, dtype):
    return jax.ShapeDtypeStruct(shape, dtype) if INTERPRET else pltpu.VMEM(shape, dtype)


VMEM = pl.BlockSpec(memory_space=pltpu.VMEM)
ANY = pl.BlockSpec(memory_space=pl.ANY)
SMEM = pl.BlockSpec(memory_space=pltpu.SMEM)


def swaps(pairs):
    return [pair for a, b in pairs for pair in ((a, b), (b, a))]


def on_device(slc_stack, fir_taps, look_index, shrink_level, window_half, basis):
    date_local, rows, cols = slc_stack.shape[1:]
    groups = lax.axis_size("date")
    slabs = lax.axis_size("az")
    block_rows = rows // groups
    pixels = block_rows * cols
    bases, dates = basis.shape
    own = bases // groups

    odd = lax.axis_index("az") & 1
    last = jnp.swapaxes(slc_stack[:, :, rows - REACH :, :], 1, 2)
    start = jnp.swapaxes(slc_stack[:, :, :REACH, :], 1, 2)
    far = lax.ppermute(
        jnp.where(odd == 0, start, last),
        "az",
        swaps([(i, i + 1) for i in range(1, slabs - 1, 2)]),
    )
    near = lax.ppermute(
        jnp.where(odd == 0, last, start),
        "az",
        swaps([(i, i + 1) for i in range(0, slabs - 1, 2)]),
    )
    pitch = rows + 8
    shape = (groups, 2, date_local, pixels)
    blocks = pl.pallas_call(
        filter_kernel,
        out_shape=jax.ShapeDtypeStruct(shape, jnp.bfloat16),
        in_specs=[SMEM, ANY] + [VMEM] * 3,
        out_specs=ANY,
        scratch_shapes=[
            pltpu.VMEM(slc_stack.shape, jnp.bfloat16),
            pltpu.VMEM((date_local * pitch, cols), jnp.float32),
            pltpu.VMEM(shape, jnp.bfloat16),
            pltpu.SemaphoreType.DMA((2,)),
            pltpu.SemaphoreType.DMA((8,)),
        ],
        interpret=INTERPRET,
        name="azimuth_filter",
    )(odd.reshape(1, 1), slc_stack, on_chip(near), on_chip(far), fir_taps)
    pix = lax.all_to_all(blocks, "date", split_axis=0, concat_axis=0, tiled=True)

    date = lax.axis_index("date").reshape(1, 1)
    look = look_index.reshape(1, -1)
    slots = 3 * block_rows
    stage, edge = pl.pallas_call(
        link_kernel,
        out_shape=(
            chip_out((slots, bases, cols), jnp.float32),
            chip_out((2 * REACH, bases, cols), jnp.bfloat16),
        ),
        in_specs=[SMEM] + [VMEM] * 5,
        out_specs=(VMEM, VMEM),
        scratch_shapes=[pltpu.VMEM((2 * (REACH + 1) * bases, pixels), jnp.float32)],
        interpret=INTERPRET,
        name="phase_link",
    )(
        date,
        on_chip(pix),
        jnp.concatenate([look, look], 1),
        shrink_level,
        window_half.reshape(1, dates),
        basis,
    )
    edge = lax.ppermute(
        edge,
        ("date", "az"),
        swaps([((groups - 1) * slabs + a, a + 1) for a in range(slabs - 1)]),
    )
    lent = pl.pallas_call(
        pack_kernel,
        out_shape=chip_out((groups, 3 * own * block_rows, cols), jnp.bfloat16),
        in_specs=[SMEM, VMEM, VMEM],
        out_specs=VMEM,
        scratch_shapes=[pltpu.VMEM((slots * bases, cols), jnp.float32)],
        interpret=INTERPRET,
        name="pack_rows",
    )(date, on_chip(stage), on_chip(edge))
    parts = lax.all_to_all(lent, "date", split_axis=0, concat_axis=0, tiled=True)
    return pl.pallas_call(
        join_kernel,
        out_shape=jax.ShapeDtypeStruct((own, 2, rows, cols), jnp.float32),
        in_specs=[VMEM],
        out_specs=VMEM,
        interpret=INTERPRET,
        name="overlap_add",
    )(on_chip(parts))


def solution(mesh):
    in_specs = (
        P(None, "date", "az", None),
        P("date", None),
        P("az", "date", None),
        P("az", "date"),
        P(),
        P(),
    )
    out_specs = P("date", None, "az", None)
    return jax.shard_map(
        on_device, mesh=mesh, in_specs=in_specs, out_specs=out_specs, check_vma=False
    )
```

time: 85.9 us -> 79 us (0.920)
  waiting for transfers between devices: 34.4 us -> 29.5 us
  starting transfers between devices: 25.3 us -> 21.4 us
  blocking collectives: 14 us -> 16 us
    ppermute x4 -> x3, waiting for transfers between devices: 13.9 us -> 8.29 us  [the longest x1 4.96 us: on_device(): lax.ppermute(edge, ('date', 'az'), swaps([((groups - 1) * slabs + a, a +...]
    ppermute x4 -> x3, starting transfers between devices: 15 us -> 10.2 us  [the longest x1 5.24 us: on_device(): lax.ppermute(jnp.where(odd == 0, start, last), 'az', swaps([(i, i + 1) fo...]
    all_to_all x1, blocking collectives: 14 us -> 16 us  [on_device(): lax.all_to_all(lent, 'date', split_axis=0, concat_axis=0, tiled=True)]
    all_to_all x1, starting transfers between devices: 10.3 us -> 11.2 us  [on_device(): lax.all_to_all(blocks, 'date', split_axis=0, concat_axis=0, tiled=True)]
    pallas_call x2 -> x3, Pallas kernels: 7.36 us -> 7.25 us  [the longest x1 3.6 us: on_device(): pl.pallas_call(link_kernel, out_shape=(chip_out((slots, bases, cols), jnp...]
  transfers between devices with their start and end apart: 5 -> 4, of which waited for: 3 -> 3; matrix products, arithmetic and copies ran while one was open for 1% -> 2% of each run, Pallas kernels for 0% -> 0%
where the time goes in v3:
time: 79 us; the launch traced here: 78.5 us
  waiting for transfers between devices  29.5 us (37%)
  starting transfers between devices  21.4 us (27%)
  blocking collectives  16 us (20%)
  Pallas kernels  8.01 us (10%)
  local copies, waits for them, and re-layouts  2.24 us (3%)
    all_to_all x1, waiting for transfers between devices, on_device(): lax.all_to_all(blocks, 'date', split_axis=0, concat_axis=0, tiled=True)  21.3 us
    all_to_all x1, blocking collectives, on_device(): lax.all_to_all(lent, 'date', split_axis=0, concat_axis=0, tiled=True)  16 us
    all_to_all x1, starting transfers between devices, on_device(): lax.all_to_all(blocks, 'date', split_axis=0, concat_axis=0, tiled=True)  11.2 us
    ppermute x1, starting transfers between devices, on_device(): lax.ppermute(jnp.where(odd == 0, start, last), 'az', swaps([(i, i + 1) fo...  5.24 us
    ppermute x1, waiting for transfers between devices, on_device(): lax.ppermute(edge, ('date', 'az'), swaps([((groups - 1) * slabs + a, a +...  4.96 us
    pallas_call x1, Pallas kernels, on_device(): pl.pallas_call(link_kernel, out_shape=(chip_out((slots, bases, cols), jnp...  3.6 us
    pallas_call x1, Pallas kernels, on_device(): pl.pallas_call(filter_kernel, out_shape=jax.ShapeDtypeStruct(shape, jnp.b...  3.4 us
    ppermute x1, waiting for transfers between devices, on_device(): lax.ppermute(jnp.where(odd == 0, start, last), 'az', swaps([(i, i + 1) fo...  3.33 us
  transfers between devices with their start and end apart: 4, of which 3 were waited for; matrix products, arithmetic and copies ran while one was open for 2% of the time, Pallas kernels for 0%

profile of v3, /device:TPU:23, one launch (start us, length us, event | category | flops | bytes accessed | tf_op | source)
XLA Modules:
  0.0 78.5 jit_solution(11396880917609696737)
XLA Ops:
  0.0 0.9 %fusion = (bf16[2,16,2,128]{3,2,1,0:T(2,128)(2,1)S(1)}, bf16[2,16,2,128]{3,2,1,0:T(2,128)(2,1)S(1)}) fusion(bf16[2,16,128,128]{3,2,1,0:T(8,128)(2,1)} %slc_hbm.1), kind=kLoop, calls=%fused_computation.3 | loop fusion | bytes 65536 | tf_op jit(solution)/shard_map/slice | solution.py:288
  0.9 0.0 copy-start
  0.9 2.6 %collective-permute-start = (bf16[2,2,16,128]{3,2,1,0:T(8,128)(2,1)S(1)}, bf16[2,2,16,128]{3,2,1,0:T(8,128)(2,1)S(1)}, u32[]{:S(2)}, u32[]{:S(2)}) collective-permute-start(bf16[2,2,16,128]{3,2,1,0:T(8,128)(2,1)S(1)} %get-tuple-element.12), channel_id=1, source_target_pairs={{0,1},{1,0},{2,3},{3,2},{4,5},{5,4},{6,7},{7,6},{8,9},{9,8},{10,11... | collective-permute-start | bytes 49160 | tf_op jit(solution)/shard_map/ppermute | solution.py:295
  3.5 5.2 %collective-permute-start.1 = (bf16[2,2,16,128]{3,2,1,0:T(8,128)(2,1)S(1)}, bf16[2,2,16,128]{3,2,1,0:T(8,128)(2,1)S(1)}, u32[]{:S(2)}, u32[]{:S(2)}) collective-permute-start(bf16[2,2,16,128]{3,2,1,0:T(8,128)(2,1)S(1)} %get-tuple-element.11), channel_id=1, source_target_pairs={{1,2},{2,1},{3,4},{4,3},{5,6},{6,5},{7,8},{8,7},{9,10},{10,9},{11,... | collective-permute-start | bytes 49160 | tf_op jit(solution)/shard_map/ppermute | solution.py:290
  8.8 0.0 copy-done
  8.8 0.7 copy.9.taps_ref
  9.5 0.0 collective-permute-done.near_ref
  9.5 3.3 %collective-permute-done.1.far_ref = bf16[2,2,16,128]{3,2,1,0:T(8,128)(2,1)S(1)} collective-permute-done((bf16[2,2,16,128]{3,2,1,0:T(8,128)(2,1)S(1)}, bf16[2,2,16,128]{3,2,1,0:T(8,128)(2,1)S(1)}, u32[]{:S(2)}, u32[]{:S(2)}) %collective-permute-start.1) | collective-permute-done | bytes 16416 | tf_op jit(solution)/shard_map/ppermute | solution.py:290
  12.8 3.4 %azimuth_filter.1 = bf16[16,2,16,1024]{3,2,1,0:T(8,128)(2,1)} custom-call(s32[1,1]{1,0:T(1,128)} %bitcast.1.odd_ref, bf16[2,16,128,128]{3,2,1,0:T(8,128)(2,1)} %slc_hbm.1, bf16[2,2,16,128]{3,2,1,0:T(8,128)(2,1)S(1)} %collective-permute-done.near_ref, bf16[2,2,16,128]{3,2,1,0:T(8,128)(2,1)S(1)} %collective-permute-done.1.far_ref, f32[16,5]{1,0:T(8,128)} %copy.9.taps_ref), custom_call_target="tpu_custom_call" | custom-call | tf_op jit(solution)/shard_map/azimuth_filter/pallas_call | solution.py:302
  16.2 11.2 %all-to-all-start = ((bf16[16,2,16,1024]{3,2,1,0:T(8,128)(2,1)}), bf16[16,2,16,1024]{3,2,1,0:T(8,128)(2,1)S(1)}, u32[]{:S(2)}, u32[]{:S(2)}) async-start(bf16[16,2,16,1024]{3,2,1,0:T(8,128)(2,1)} %azimuth_filter.1), calls=%async_computation | async-start | bytes 2097152 | tf_op jit(solution)/shard_map/all_to_all | solution.py:317
  28.0 0.0 copy-start.1
  28.1 0.6 copy-done.1
  28.7 0.6 pad_add_fusion.look_ref
  29.3 21.3 %all-to-all-done.pix_ref = bf16[16,2,16,1024]{3,2,1,0:T(8,128)(2,1)S(1)} async-done(((bf16[16,2,16,1024]{3,2,1,0:T(8,128)(2,1)}), bf16[16,2,16,1024]{3,2,1,0:T(8,128)(2,1)S(1)}, u32[]{:S(2)}, u32[]{:S(2)}) %all-to-all-start) | async-done | bytes 1048608 | tf_op jit(solution)/shard_map/all_to_all | solution.py:317
  50.6 3.6 %phase_link.1 = (f32[24,32,128]{2,1,0:T(8,128)S(1)}, bf16[4,32,128]{2,1,0:T(8,128)(2,1)S(1)}) custom-call(s32[1,1]{1,0:T(1,128)} %bitcast.date_ref, bf16[16,2,16,1024]{3,2,1,0:T(8,128)(2,1)S(1)} %all-to-all-done.pix_ref, s32[1,128]{1,0:T(1,128)} %pad_add_fusion.look_ref, s32[1,1]{1,0:T(1,128)S(6)} %copy.16.level_ref, s32[1,256]{1,0:T(1,128)} %bitcast.8, ...), custom_call_target="tpu_custom_call" | custom-call | tf_op jit(solution)/shard_map/phase_link/pallas_call | solution.py:322
  54.2 2.4 %collective-permute-start.2 = (bf16[4,32,128]{2,1,0:T(8,128)(2,1)S(1)}, bf16[4,32,128]{2,1,0:T(8,128)(2,1)S(1)}, u32[]{:S(2)}, u32[]{:S(2)}) collective-permute-start(bf16[4,32,128]{2,1,0:T(8,128)(2,1)S(1)} %get-tuple-element.8), channel_id=1, source_target_pairs={{480,1},{1,480},{481,2},{2,481},{482,3},{3,482},{483,4},{4,483},{4... | collective-permute-start | bytes 98312 | tf_op jit(solution)/shard_map/ppermute | solution.py:341
  56.6 5.0 %collective-permute-done.2.edge_ref = bf16[4,32,128]{2,1,0:T(8,128)(2,1)S(1)} collective-permute-done((bf16[4,32,128]{2,1,0:T(8,128)(2,1)S(1)}, bf16[4,32,128]{2,1,0:T(8,128)(2,1)S(1)}, u32[]{:S(2)}, u32[]{:S(2)}) %collective-permute-start.2) | collective-permute-done | bytes 32800 | tf_op jit(solution)/shard_map/ppermute | solution.py:341
  61.5 0.2 pack_rows.1
  61.8 16.0 %all_to_all.10.part_ref = bf16[16,48,128]{2,1,0:T(8,128)(2,1)S(1)} all-to-all(bf16[16,48,128]{2,1,0:T(8,128)(2,1)S(1)} %pack_rows.1), channel_id=1, replica_groups=mesh['date'=16,'az'=32] {'date'}, dimensions={0} | all-to-all | bytes 393216 | tf_op jit(solution)/shard_map/all_to_all | solution.py:355
  77.7 0.8 overlap_add.1
  (1 shorter events, 0.0 us)
Async XLA Ops:
  0.9 7.9 %copy-start = (f32[16,5]{0,1:T(8,128)S(1)}, f32[16,5]{0,1:T(8,128)}, u32[]{:S(2)}) copy-start(f32[16,5]{0,1:T(8,128)} %param.7) | copy-start | bytes 964
  0.9 8.5 %collective-permute-start = (bf16[2,2,16,128]{3,2,1,0:T(8,128)(2,1)S(1)}, bf16[2,2,16,128]{3,2,1,0:T(8,128)(2,1)S(1)}, u32[]{:S(2)}, u32[]{:S(2)}) collective-permute-start(bf16[2,2,16,128]{3,2,1,0:T(8,128)(2,1)S(1)} %get-tuple-element.12), channel_id=1, source_target_pairs={{0,1},{1,0},{2,3},{3,2},{4,5},{5,4},{6,7},{7,6},{8,9},{9,8},{10,11... | collective-permute-start | bytes 49160 | tf_op jit(solution)/shard_map/ppermute | solution.py:295
  3.5 9.3 %collective-permute-start.1 = (bf16[2,2,16,128]{3,2,1,0:T(8,128)(2,1)S(1)}, bf16[2,2,16,128]{3,2,1,0:T(8,128)(2,1)S(1)}, u32[]{:S(2)}, u32[]{:S(2)}) collective-permute-start(bf16[2,2,16,128]{3,2,1,0:T(8,128)(2,1)S(1)} %get-tuple-element.11), channel_id=1, source_target_pairs={{1,2},{2,1},{3,4},{4,3},{5,6},{6,5},{7,8},{8,7},{9,10},{10,9},{11,... | collective-permute-start | bytes 49160 | tf_op jit(solution)/shard_map/ppermute | solution.py:290
  16.2 34.4 %all-to-all-start = ((bf16[16,2,16,1024]{3,2,1,0:T(8,128)(2,1)}), bf16[16,2,16,1024]{3,2,1,0:T(8,128)(2,1)S(1)}, u32[]{:S(2)}, u32[]{:S(2)}) async-start(bf16[16,2,16,1024]{3,2,1,0:T(8,128)(2,1)} %azimuth_filter.1), calls=%async_computation | async-start | bytes 2097152 | tf_op jit(solution)/shard_map/all_to_all | solution.py:317
  28.0 0.7 copy-start.1
  54.2 7.3 %collective-permute-start.2 = (bf16[4,32,128]{2,1,0:T(8,128)(2,1)S(1)}, bf16[4,32,128]{2,1,0:T(8,128)(2,1)S(1)}, u32[]{:S(2)}, u32[]{:S(2)}) collective-permute-start(bf16[4,32,128]{2,1,0:T(8,128)(2,1)S(1)} %get-tuple-element.8), channel_id=1, source_target_pairs={{480,1},{1,480},{481,2},{2,481},{482,3},{3,482},{483,4},{4,483},{4... | collective-permute-start | bytes 98312 | tf_op jit(solution)/shard_map/ppermute | solution.py:341

commit v4 on v3

--- a/solution.py
+++ b/solution.py
@@ -11,24 +11,46 @@
 
 
 def filter_kernel(
-    odd_ref, slc_hbm, near_ref, far_ref, taps_ref, out_ref, slc_ref, held, done, load_sems, sems
+    slc_hbm,
+    near_ref,
+    far_ref,
+    taps_ref,
+    look_hbm,
+    level_smem,
+    half_hbm,
+    basis_hbm,
+    out_ref,
+    look_ref,
+    level_ref,
+    half_ref,
+    basis_ref,
+    slc_ref,
+    held,
+    sems,
 ):
     _, dates, rows, cols = slc_ref.shape
     blocks = out_ref.shape[0]
     block_rows = rows // blocks
     pitch = held.shape[0] // dates
-    even = odd_ref[0, 0] == 0
+    even = (lax.axis_index("az") & 1) == 0
+    columns = taps_ref[...].T
     taps = [
-        jnp.broadcast_to(taps_ref[:, j : j + 1], (dates, cols)) for j in range(2 * REACH + 1)
+        jnp.broadcast_to(columns[:, j : j + 1], (dates, cols)) for j in range(2 * REACH + 1)
     ]
-    parts = sems.shape[0] // 2
-    share = blocks // parts
-    copies = []
     loads = [
-        pltpu.make_async_copy(slc_hbm.at[c], slc_ref.at[c], load_sems.at[c]) for c in range(2)
+        pltpu.make_async_copy(slc_hbm.at[c], slc_ref.at[c], sems.at[c]) for c in range(2)
     ]
-    for load in loads:
-        load.start()
+    small = [
+        (look_hbm, look_ref),
+        (half_hbm, half_ref),
+        (basis_hbm, basis_ref),
+    ]
+    copies = [
+        pltpu.make_async_copy(a, b, sems.at[2 + i]) for i, (a, b) in enumerate(small)
+    ]
+    for copy in loads + copies:
+        copy.start()
+    level_ref[...] = jnp.full(level_ref.shape, level_smem[0, 0].astype(jnp.float32))
     for c in range(2):
         loads[c].wait()
         for t in range(dates):
@@ -51,16 +73,7 @@
                 total = total + taps[j] * window[j]
             window.pop(0)
             b, i = divmod(r, block_rows)
-            done[b, c, :, i * cols : (i + 1) * cols] = total.astype(jnp.bfloat16)
-            if (r + 1) % (share * block_rows) == 0:
-                part = b // share
-                copy = pltpu.make_async_copy(
-                    done.at[pl.ds(part * share, share), c],
-                    out_ref.at[pl.ds(part * share, share), c],
-                    sems.at[c * parts + part],
-                )
-                copy.start()
-                copies.append(copy)
+            out_ref[b, c, :, i * cols : (i + 1) * cols] = total.astype(jnp.bfloat16)
     for copy in copies:
         copy.wait()
 
@@ -87,17 +100,18 @@
 
 
 def link_kernel(
-    date_ref, pix_ref, look_ref, level_ref, half_ref, basis_ref, stage_ref, edge_ref, proj
+    pix_ref, look_ref, level_ref, half_ref, basis_ref, stage_ref, edge_ref, proj
 ):
     groups, _, dates_own, pixels = pix_ref.shape
     dates = groups * dates_own
-    width = look_ref.shape[1]
-    looks = width // 2
+    looks = look_ref.shape[1]
+    width = 2 * looks
     bases = basis_ref.shape[0]
     cols = stage_ref.shape[2]
     block_rows = pixels // cols
     place = lax.broadcasted_iota(jnp.int32, (pixels, width), 0)
-    picked = (place == look_ref[...]).astype(jnp.float32).astype(jnp.bfloat16)
+    chosen = jnp.concatenate([look_ref[...], look_ref[...]], 1)
+    picked = (place == chosen).astype(jnp.float32).astype(jnp.bfloat16)
     samp_re = dot(pix_ref[:, 0].reshape(dates, pixels), picked)
     samp_im = dot(pix_ref[:, 1].reshape(dates, pixels), picked)
     first = lax.broadcasted_iota(jnp.int32, (dates, width), 1) < looks
@@ -127,7 +141,7 @@
     trace = total(inner * identity)
     square = total(inner * inner)
     mean = trace / (looks * dates) + 1e-06
-    weight = level_ref[...].astype(jnp.float32) / 16.0
+    weight = level_ref[:, :1] / 16.0
     alpha = weight * mean + mean
     beta = (1.0 - weight) / looks
     scale = 1.0 / jnp.sqrt(
@@ -170,7 +184,7 @@
     slots += [(0, r) for r in below] + [(1, r) for r in below]
     slots += [(1, r) for r in above] + [(0, r) for r in above]
     sub = 8
-    opens = date_ref[0, 0] == 0
+    opens = lax.axis_index("date") == 0
     for k in range(0, bases, sub):
         rest = {}
         for c in range(2):
@@ -200,13 +214,13 @@
             edge_ref[i, pl.ds(k, sub), :] = edge.astype(jnp.bfloat16)
 
 
-def pack_kernel(date_ref, stage_ref, edge_ref, out_ref, held):
+def pack_kernel(stage_ref, edge_ref, out_ref, held):
     groups = out_ref.shape[0]
     slots, bases, cols = stage_ref.shape
     sub = slots // 3
     own = bases // groups
-    opens = date_ref[0, 0] == 0
-    closes = date_ref[0, 0] == groups - 1
+    opens = lax.axis_index("date") == 0
+    closes = lax.axis_index("date") == groups - 1
     for q in range(slots):
         value = stage_ref[q]
         i = q - 2 * sub
@@ -243,14 +257,11 @@
             for c in range(2):
                 start = (k * 2 + c) * block_rows
                 main = part_ref[b, start : start + block_rows, :].astype(jnp.float32)
-                if b:
-                    before = pltpu.roll(lends[b - 1], block_rows - 2, 0) if c else lends[b - 1]
-                else:
-                    before = pltpu.roll(lends[0], 2 if c else 4, 0)
-                if b < groups - 1:
-                    after = pltpu.roll(lends[b + 1], 2, 0) if c else lends[b + 1]
-                else:
-                    after = pltpu.roll(lends[b], block_rows - 2 if c else 4, 0)
+                before = lends[b - 1]
+                after = lends[(b + 1) % groups]
+                if c == 1:
+                    before = pltpu.roll(before, block_rows - 2, 0)
+                    after = pltpu.roll(after, 2, 0)
                 out_ref[k, c, b * block_rows : (b + 1) * block_rows, :] = (
                     main
                     + jnp.where(sub < 2, before, 0.0)
@@ -299,25 +310,38 @@
     )
     pitch = rows + 8
     shape = (groups, 2, date_local, pixels)
-    blocks = pl.pallas_call(
+    look = look_index.reshape(1, -1)
+    half = window_half.reshape(1, dates)
+    blocks, look, level, half, basis = pl.pallas_call(
         filter_kernel,
-        out_shape=jax.ShapeDtypeStruct(shape, jnp.bfloat16),
-        in_specs=[SMEM, ANY] + [VMEM] * 3,
-        out_specs=ANY,
+        out_shape=(
+            chip_out(shape, jnp.bfloat16),
+            chip_out(look.shape, look.dtype),
+            chip_out((1, cols), jnp.float32),
+            chip_out(half.shape, half.dtype),
+            chip_out(basis.shape, basis.dtype),
+        ),
+        in_specs=[ANY] + [VMEM] * 3 + [ANY, SMEM, ANY, ANY],
+        out_specs=(VMEM,) * 5,
         scratch_shapes=[
             pltpu.VMEM(slc_stack.shape, jnp.bfloat16),
             pltpu.VMEM((date_local * pitch, cols), jnp.float32),
-            pltpu.VMEM(shape, jnp.bfloat16),
-            pltpu.SemaphoreType.DMA((2,)),
-            pltpu.SemaphoreType.DMA((8,)),
+            pltpu.SemaphoreType.DMA((5,)),
         ],
         interpret=INTERPRET,
         name="azimuth_filter",
-    )(odd.reshape(1, 1), slc_stack, on_chip(near), on_chip(far), fir_taps)
+    )(
+        slc_stack,
+        on_chip(near),
+        on_chip(far),
+        on_chip(fir_taps.T),
+        look,
+        shrink_level,
+        half,
+        basis,
+    )
     pix = lax.all_to_all(blocks, "date", split_axis=0, concat_axis=0, tiled=True)
 
-    date = lax.axis_index("date").reshape(1, 1)
-    look = look_index.reshape(1, -1)
     slots = 3 * block_rows
     stage, edge = pl.pallas_call(
         link_kernel,
@@ -325,33 +349,33 @@
             chip_out((slots, bases, cols), jnp.float32),
             chip_out((2 * REACH, bases, cols), jnp.bfloat16),
         ),
-        in_specs=[SMEM] + [VMEM] * 5,
+        in_specs=[VMEM] * 5,
         out_specs=(VMEM, VMEM),
         scratch_shapes=[pltpu.VMEM((2 * (REACH + 1) * bases, pixels), jnp.float32)],
         interpret=INTERPRET,
         name="phase_link",
     )(
-        date,
         on_chip(pix),
-        jnp.concatenate([look, look], 1),
-        shrink_level,
-        window_half.reshape(1, dates),
-        basis,
+        on_chip(look),
+        on_chip(level),
+        on_chip(half),
+        on_chip(basis),
     )
     edge = lax.ppermute(
         edge,
         ("date", "az"),
-        swaps([((groups - 1) * slabs + a, a + 1) for a in range(slabs - 1)]),
+        [((groups - 1) * slabs + a, (groups - 1) * slabs + a + 1) for a in range(slabs - 1)]
+        + [(a + 1, a) for a in range(slabs - 1)],
     )
     lent = pl.pallas_call(
         pack_kernel,
         out_shape=chip_out((groups, 3 * own * block_rows, cols), jnp.bfloat16),
-        in_specs=[SMEM, VMEM, VMEM],
+        in_specs=[VMEM, VMEM],
         out_specs=VMEM,
         scratch_shapes=[pltpu.VMEM((slots * bases, cols), jnp.float32)],
         interpret=INTERPRET,
         name="pack_rows",
-    )(date, on_chip(stage), on_chip(edge))
+    )(on_chip(stage), on_chip(edge))
     parts = lax.all_to_all(lent, "date", split_axis=0, concat_axis=0, tiled=True)
     return pl.pallas_call(
         join_kernel,

time: 79 us -> 77.7 us (0.984)
  the two profiles are of different devices: /device:TPU:23 before, /device:TPU:40 now
where the time goes in v4:
time: 77.7 us; the launch traced here: 77.4 us
  blocking collectives  60.6 us (78%)
  starting transfers between devices  7.36 us (9%)
  Pallas kernels  5.95 us (8%)
  waiting for transfers between devices  1.91 us (2%)
  local copies, waits for them, and re-layouts  0.91 us (1%)
    all_to_all x1, blocking collectives, on_device(): lax.all_to_all(blocks, 'date', split_axis=0, concat_axis=0, tiled=True)  38.3 us
    all_to_all x1, blocking collectives, on_device(): lax.all_to_all(lent, 'date', split_axis=0, concat_axis=0, tiled=True)  22.2 us
    ppermute x1, starting transfers between devices, on_device(): lax.ppermute(jnp.where(odd == 0, start, last), 'az', swaps([(i, i + 1) fo...  4.78 us
    pallas_call x1, Pallas kernels, on_device(): pl.pallas_call(link_kernel, out_shape=(chip_out((slots, bases, cols), jnp...  2.93 us
    pallas_call x1, Pallas kernels, on_device(): pl.pallas_call(filter_kernel, out_shape=(chip_out(shape, jnp.bfloat16), c...  2.01 us
    ppermute x1, starting transfers between devices, on_device(): lax.ppermute(jnp.where(odd == 0, last, start), 'az', swaps([(i, i + 1) fo...  1.92 us
    ppermute x1, waiting for transfers between devices, on_device(): lax.ppermute(jnp.where(odd == 0, start, last), 'az', swaps([(i, i + 1) fo...  1.9 us
  transfers between devices with their start and end apart: 3, of which 1 were waited for; matrix products, arithmetic and copies ran while one was open for 0% of the time, Pallas kernels for 0%

profile of v4, /device:TPU:40, one launch (start us, length us, event | category | flops | bytes accessed | tf_op | source)
XLA Modules:
  0.0 77.4 jit_solution(6719267802771998494)
XLA Ops:
  0.0 0.9 %fusion = (bf16[2,16,2,128]{3,2,1,0:T(2,128)(2,1)S(1)}, bf16[2,16,2,128]{3,2,1,0:T(2,128)(2,1)S(1)}) fusion(bf16[2,16,128,128]{3,2,1,0:T(8,128)(2,1)} %slc_hbm.1), kind=kLoop, calls=%fused_computation.2 | loop fusion | bytes 65536 | tf_op jit(solution)/shard_map/slice | solution.py:299
  0.9 4.8 %collective-permute-start.1 = (bf16[2,2,16,128]{3,2,1,0:T(8,128)(2,1)S(1)}, bf16[2,2,16,128]{3,2,1,0:T(8,128)(2,1)S(1)}, u32[]{:S(2)}, u32[]{:S(2)}) collective-permute-start(bf16[2,2,16,128]{3,2,1,0:T(8,128)(2,1)S(1)} %get-tuple-element.21), channel_id=1, source_target_pairs={{1,2},{2,1},{3,4},{4,3},{5,6},{6,5},{7,8},{8,7},{9,10},{10,9},{11,... | collective-permute-start | bytes 49160 | tf_op jit(solution)/shard_map/ppermute | solution.py:301
  5.7 0.0 copy-start
  5.7 1.9 %collective-permute-start = (bf16[2,2,16,128]{3,2,1,0:T(8,128)(2,1)S(1)}, bf16[2,2,16,128]{3,2,1,0:T(8,128)(2,1)S(1)}, u32[]{:S(2)}, u32[]{:S(2)}) collective-permute-start(bf16[2,2,16,128]{3,2,1,0:T(8,128)(2,1)S(1)} %get-tuple-element.22), channel_id=1, source_target_pairs={{0,1},{1,0},{2,3},{3,2},{4,5},{5,4},{6,7},{7,6},{8,9},{9,8},{10,11... | collective-permute-start | bytes 49160 | tf_op jit(solution)/shard_map/ppermute | solution.py:306
  8.3 1.9 %collective-permute-done.1.far_ref = bf16[2,2,16,128]{3,2,1,0:T(8,128)(2,1)S(1)} collective-permute-done((bf16[2,2,16,128]{3,2,1,0:T(8,128)(2,1)S(1)}, bf16[2,2,16,128]{3,2,1,0:T(8,128)(2,1)S(1)}, u32[]{:S(2)}, u32[]{:S(2)}) %collective-permute-start.1) | collective-permute-done | bytes 16416 | tf_op jit(solution)/shard_map/ppermute | solution.py:301
  10.2 0.0 collective-permute-done.near_ref
  10.2 0.0 copy-done
  10.2 2.0 %azimuth_filter.1 = (bf16[16,2,16,1024]{3,2,1,0:T(8,128)(2,1)S(1)}, s32[1,64]{1,0:T(1,128)S(1)}, f32[1,128]{1,0:T(1,128)S(1)}, s32[1,256]{1,0:T(1,128)S(1)}, bf16[32,256]{1,0:T(8,128)(2,1)S(1)}) custom-call(bf16[2,16,128,128]{3,2,1,0:T(8,128)(2,1)} %slc_hbm.1, bf16[2,2,16,128]{3,2,1,0:T(8,128)(2,1)S(1)} %collective-permute-done.near_ref, ...), custom_call_target="tpu_custom_call" | custom-call | tf_op jit(solution)/shard_map/azimuth_filter/pallas_call | solution.py:315
  12.2 38.3 %all_to_all.10.pix_ref = bf16[16,2,16,1024]{3,2,1,0:T(8,128)(2,1)S(1)} all-to-all(bf16[16,2,16,1024]{3,2,1,0:T(8,128)(2,1)S(1)} %get-tuple-element.12), channel_id=1, replica_groups=mesh['date'=16,'az'=32] {'date'}, dimensions={0} | all-to-all | bytes 2097152 | tf_op jit(solution)/shard_map/all_to_all | solution.py:343
  50.6 2.9 %phase_link.1 = (f32[24,32,128]{2,1,0:T(8,128)S(1)}, bf16[4,32,128]{2,1,0:T(8,128)(2,1)S(1)}) custom-call(bf16[16,2,16,1024]{3,2,1,0:T(8,128)(2,1)S(1)} %all_to_all.10.pix_ref, s32[1,64]{1,0:T(1,128)S(1)} %get-tuple-element.13.look_ref, f32[1,128]{1,0:T(1,128)S(1)} %get-tuple-element.14.level_ref, s32[1,256]{1,0:T(1,128)S(1)} %get-tuple-element.15.half_ref, ...), custom_call_target="tpu_custom_call" | custom-call | tf_op jit(solution)/shard_map/phase_link/pallas_call | solution.py:346
  53.5 0.7 collective-permute-start.2
  54.2 0.0 collective-permute-done.2.edge_ref
  54.2 0.3 pack_rows.1
  54.4 22.2 %all_to_all.11.part_ref = bf16[16,48,128]{2,1,0:T(8,128)(2,1)S(1)} all-to-all(bf16[16,48,128]{2,1,0:T(8,128)(2,1)S(1)} %pack_rows.1), channel_id=1, replica_groups=mesh['date'=16,'az'=32] {'date'}, dimensions={0} | all-to-all | bytes 393216 | tf_op jit(solution)/shard_map/all_to_all | solution.py:379
  76.7 0.8 overlap_add.1
  (1 shorter events, 0.0 us)
Async XLA Ops:
  0.9 9.3 %collective-permute-start.1 = (bf16[2,2,16,128]{3,2,1,0:T(8,128)(2,1)S(1)}, bf16[2,2,16,128]{3,2,1,0:T(8,128)(2,1)S(1)}, u32[]{:S(2)}, u32[]{:S(2)}) collective-permute-start(bf16[2,2,16,128]{3,2,1,0:T(8,128)(2,1)S(1)} %get-tuple-element.21), channel_id=1, source_target_pairs={{1,2},{2,1},{3,4},{4,3},{5,6},{6,5},{7,8},{8,7},{9,10},{10,9},{11,... | collective-permute-start | bytes 49160 | tf_op jit(solution)/shard_map/ppermute | solution.py:301
  5.7 4.5 %copy-start = (f32[16,5]{0,1:T(8,128)S(1)}, f32[16,5]{0,1:T(8,128)}, u32[]{:S(2)}) copy-start(f32[16,5]{0,1:T(8,128)} %param.7) | copy-start | bytes 964
  5.7 4.5 %collective-permute-start = (bf16[2,2,16,128]{3,2,1,0:T(8,128)(2,1)S(1)}, bf16[2,2,16,128]{3,2,1,0:T(8,128)(2,1)S(1)}, u32[]{:S(2)}, u32[]{:S(2)}) collective-permute-start(bf16[2,2,16,128]{3,2,1,0:T(8,128)(2,1)S(1)} %get-tuple-element.22), channel_id=1, source_target_pairs={{0,1},{1,0},{2,3},{3,2},{4,5},{5,4},{6,7},{7,6},{8,9},{9,8},{10,11... | collective-permute-start | bytes 49160 | tf_op jit(solution)/shard_map/ppermute | solution.py:306
  53.5 0.7 collective-permute-start.2

commit v5 on v4

--- a/solution.py
+++ b/solution.py
@@ -5,21 +5,36 @@
 from jax.experimental.pallas import tpu as pltpu
 from jax.sharding import PartitionSpec as P
 
+
 NS_ITERS = 6
 REACH = 2
 INTERPRET = False
 
 
+def spread(taps_ref, cols):
+    columns = taps_ref[...].T
+    return [
+        jnp.broadcast_to(columns[:, j : j + 1], (columns.shape[0], cols))
+        for j in range(2 * REACH + 1)
+    ]
+
+
+def weigh(taps, window):
+    total = taps[0] * window[0]
+    for j in range(1, 2 * REACH + 1):
+        total = total + taps[j] * window[j]
+    return total.astype(jnp.bfloat16)
+
+
 def filter_kernel(
     slc_hbm,
-    near_ref,
-    far_ref,
     taps_ref,
     look_hbm,
     level_smem,
     half_hbm,
     basis_hbm,
     out_ref,
+    rim_ref,
     look_ref,
     level_ref,
     half_ref,
@@ -32,11 +47,7 @@
     blocks = out_ref.shape[0]
     block_rows = rows // blocks
     pitch = held.shape[0] // dates
-    even = (lax.axis_index("az") & 1) == 0
-    columns = taps_ref[...].T
-    taps = [
-        jnp.broadcast_to(columns[:, j : j + 1], (dates, cols)) for j in range(2 * REACH + 1)
-    ]
+    taps = spread(taps_ref, cols)
     loads = [
         pltpu.make_async_copy(slc_hbm.at[c], slc_ref.at[c], sems.at[c]) for c in range(2)
     ]
@@ -57,25 +68,42 @@
             held[pl.ds(t * pitch, rows), :] = slc_ref[c, t].astype(jnp.float32)
 
         def line(r):
-            if r < 0:
-                pick = jnp.where(even, far_ref[c, r + REACH], near_ref[c, r + REACH])
-                return pick.astype(jnp.float32)
-            if r >= rows:
-                pick = jnp.where(even, near_ref[c, r - rows], far_ref[c, r - rows])
-                return pick.astype(jnp.float32)
             return held[pl.ds(r, dates, stride=pitch), :]
 
-        window = [line(r) for r in range(-REACH, REACH)]
-        for r in range(rows):
+        window = [line(r) for r in range(2 * REACH)]
+        for i in range(2 * REACH):
+            rim_ref[0, c, i] = window[i]
+        for r in range(REACH, rows - REACH):
             window.append(line(r + REACH))
-            total = taps[0] * window[0]
-            for j in range(1, 2 * REACH + 1):
-                total = total + taps[j] * window[j]
+            b, i = divmod(r, block_rows)
+            out_ref[b, c, :, i * cols : (i + 1) * cols] = weigh(taps, window)
             window.pop(0)
-            b, i = divmod(r, block_rows)
-            out_ref[b, c, :, i * cols : (i + 1) * cols] = total.astype(jnp.bfloat16)
+        for i in range(2 * REACH):
+            rim_ref[1, c, i] = window[i]
     for copy in copies:
         copy.wait()
+
+
+def rim_kernel(part_ref, rim_ref, near_ref, far_ref, taps_ref, out_ref):
+    del part_ref
+    blocks = out_ref.shape[0]
+    cols = rim_ref.shape[-1]
+    block_rows = out_ref.shape[-1] // cols
+    even = (lax.axis_index("az") & 1) == 0
+    taps = spread(taps_ref, cols)
+    for c in range(2):
+        own = [[rim_ref[side, c, i] for i in range(2 * REACH)] for side in range(2)]
+        near = [near_ref[c, i].astype(jnp.float32) for i in range(REACH)]
+        far = [far_ref[c, i].astype(jnp.float32) for i in range(REACH)]
+        low = [jnp.where(even, b, a) for a, b in zip(near, far)] + own[0]
+        high = own[1] + [jnp.where(even, a, b) for a, b in zip(near, far)]
+        for i in range(REACH):
+            window = slice(i, i + 2 * REACH + 1)
+            out_ref[0, c, :, i * cols : (i + 1) * cols] = weigh(taps, low[window])
+            row = block_rows - REACH + i
+            out_ref[blocks - 1, c, :, row * cols : (row + 1) * cols] = weigh(
+                taps, high[window]
+            )
 
 
 def split(x):
@@ -216,7 +244,7 @@
 
 def pack_kernel(stage_ref, edge_ref, out_ref, held):
     groups = out_ref.shape[0]
-    slots, bases, cols = stage_ref.shape
+    slots, bases, _ = stage_ref.shape
     sub = slots // 3
     own = bases // groups
     opens = lax.axis_index("date") == 0
@@ -312,17 +340,19 @@
     shape = (groups, 2, date_local, pixels)
     look = look_index.reshape(1, -1)
     half = window_half.reshape(1, dates)
-    blocks, look, level, half, basis = pl.pallas_call(
+    taps = fir_taps.T
+    blocks, rim, look, level, half, basis = pl.pallas_call(
         filter_kernel,
         out_shape=(
             chip_out(shape, jnp.bfloat16),
+            chip_out((2, 2, 2 * REACH, date_local, cols), jnp.float32),
             chip_out(look.shape, look.dtype),
             chip_out((1, cols), jnp.float32),
             chip_out(half.shape, half.dtype),
             chip_out(basis.shape, basis.dtype),
         ),
-        in_specs=[ANY] + [VMEM] * 3 + [ANY, SMEM, ANY, ANY],
-        out_specs=(VMEM,) * 5,
+        in_specs=[ANY, VMEM, ANY, SMEM, ANY, ANY],
+        out_specs=(VMEM,) * 6,
         scratch_shapes=[
             pltpu.VMEM(slc_stack.shape, jnp.bfloat16),
             pltpu.VMEM((date_local * pitch, cols), jnp.float32),
@@ -330,16 +360,16 @@
         ],
         interpret=INTERPRET,
         name="azimuth_filter",
-    )(
-        slc_stack,
-        on_chip(near),
-        on_chip(far),
-        on_chip(fir_taps.T),
-        look,
-        shrink_level,
-        half,
-        basis,
-    )
+    )(slc_stack, on_chip(taps), look, shrink_level, half, basis)
+    blocks = pl.pallas_call(
+        rim_kernel,
+        out_shape=chip_out(shape, jnp.bfloat16),
+        in_specs=[VMEM] * 5,
+        out_specs=VMEM,
+        input_output_aliases={0: 0},
+        interpret=INTERPRET,
+        name="filter_rim",
+    )(on_chip(blocks), on_chip(rim), on_chip(near), on_chip(far), on_chip(taps))
     pix = lax.all_to_all(blocks, "date", split_axis=0, concat_axis=0, tiled=True)
 
     slots = 3 * block_rows

time: 77.7 us -> 75.7 us (0.974)
  waiting for transfers between devices: 1.91 us -> 0.01 us
    all_to_all x1, blocking collectives: 22.2 us -> 20.2 us  [on_device(): lax.all_to_all(lent, 'date', split_axis=0, concat_axis=0, tiled=True)]
    ppermute x1, waiting for transfers between devices: 1.9 us -> 0.01 us  [on_device(): lax.ppermute(jnp.where(odd == 0, start, last), 'az', swaps([(i, i + 1) fo...]
    all_to_all x1, blocking collectives: 38.3 us -> 40 us  [on_device(): lax.all_to_all(blocks, 'date', split_axis=0, concat_axis=0, tiled=True)]
  transfers between devices with their start and end apart: 3 -> 3, of which waited for: 1 -> 0; matrix products, arithmetic and copies ran while one was open for 0% -> 0% of each run, Pallas kernels for 0% -> 3%
where the time goes in v5:
time: 75.7 us; the launch traced here: 75.4 us
  blocking collectives  60.3 us (80%)
  starting transfers between devices  7.36 us (10%)
  Pallas kernels  6.07 us (8%)
  local copies, waits for them, and re-layouts  0.91 us (1%)
  between operations  0.76 us (1%)
    all_to_all x1, blocking collectives, on_device(): lax.all_to_all(blocks, 'date', split_axis=0, concat_axis=0, tiled=True)  40 us
    all_to_all x1, blocking collectives, on_device(): lax.all_to_all(lent, 'date', split_axis=0, concat_axis=0, tiled=True)  20.2 us
    ppermute x1, starting transfers between devices, on_device(): lax.ppermute(jnp.where(odd == 0, start, last), 'az', swaps([(i, i + 1) fo...  4.78 us
    pallas_call x1, Pallas kernels, on_device(): pl.pallas_call(link_kernel, out_shape=(chip_out((slots, bases, cols), jnp...  2.92 us
    pallas_call x1, Pallas kernels, on_device(): pl.pallas_call(filter_kernel, out_shape=(chip_out(shape, jnp.bfloat16), c...  1.98 us
    ppermute x1, starting transfers between devices, on_device(): lax.ppermute(jnp.where(odd == 0, last, start), 'az', swaps([(i, i + 1) fo...  1.92 us
  transfers between devices with their start and end apart: 3, of which 0 were waited for; matrix products, arithmetic and copies ran while one was open for 0% of the time, Pallas kernels for 3%

profile of v5, /device:TPU:40, one launch (start us, length us, event | category | flops | bytes accessed | tf_op | source)
XLA Modules:
  0.0 75.4 jit_solution(13952781538422304843)
XLA Ops:
  0.0 0.9 %fusion = (bf16[2,16,2,128]{3,2,1,0:T(2,128)(2,1)S(1)}, bf16[2,16,2,128]{3,2,1,0:T(2,128)(2,1)S(1)}) fusion(bf16[2,16,128,128]{3,2,1,0:T(8,128)(2,1)} %slc_hbm.1), kind=kLoop, calls=%fused_computation.2 | loop fusion | bytes 65536 | tf_op jit(solution)/shard_map/slice | solution.py:327
  0.9 4.8 %collective-permute-start.1 = (bf16[2,2,16,128]{3,2,1,0:T(8,128)(2,1)S(1)}, bf16[2,2,16,128]{3,2,1,0:T(8,128)(2,1)S(1)}, u32[]{:S(2)}, u32[]{:S(2)}) collective-permute-start(bf16[2,2,16,128]{3,2,1,0:T(8,128)(2,1)S(1)} %get-tuple-element.23), channel_id=1, source_target_pairs={{1,2},{2,1},{3,4},{4,3},{5,6},{6,5},{7,8},{8,7},{9,10},{10,9},{11,... | collective-permute-start | bytes 49160 | tf_op jit(solution)/shard_map/ppermute | solution.py:329
  5.7 0.0 copy-start
  5.7 1.9 %collective-permute-start = (bf16[2,2,16,128]{3,2,1,0:T(8,128)(2,1)S(1)}, bf16[2,2,16,128]{3,2,1,0:T(8,128)(2,1)S(1)}, u32[]{:S(2)}, u32[]{:S(2)}) collective-permute-start(bf16[2,2,16,128]{3,2,1,0:T(8,128)(2,1)S(1)} %get-tuple-element.24), channel_id=1, source_target_pairs={{0,1},{1,0},{2,3},{3,2},{4,5},{5,4},{6,7},{7,6},{8,9},{9,8},{10,11... | collective-permute-start | bytes 49160 | tf_op jit(solution)/shard_map/ppermute | solution.py:334
  8.3 0.0 copy-done
  8.3 2.0 %azimuth_filter.1 = (bf16[16,2,16,1024]{3,2,1,0:T(8,128)(2,1)S(1)}, f32[2,2,4,16,128]{4,3,2,1,0:T(8,128)S(1)}, s32[1,64]{1,0:T(1,128)S(1)}, f32[1,128]{1,0:T(1,1...) custom-call(bf16[2,16,128,128]{3,2,1,0:T(8,128)(2,1)} %slc_hbm.1, f32[5,16]{1,0:T(8,128)S(1)} %bitcast.7, ...), custom_call_target="tpu_custom_call" | custom-call | tf_op jit(solution)/shard_map/azimuth_filter/pallas_call | solution.py:344
  10.3 0.0 collective-permute-done.1.far_ref
  10.3 0.0 collective-permute-done.near_ref
  10.3 0.2 filter_rim.1
  10.5 40.0 %all_to_all.10.pix_ref = bf16[16,2,16,1024]{3,2,1,0:T(8,128)(2,1)S(1)} all-to-all(bf16[16,2,16,1024]{3,2,1,0:T(8,128)(2,1)S(1)} %filter_rim.1), channel_id=1, replica_groups=mesh['date'=16,'az'=32] {'date'}, dimensions={0} | all-to-all | bytes 2097152 | tf_op jit(solution)/shard_map/all_to_all | solution.py:373
  50.5 2.9 %phase_link.1 = (f32[24,32,128]{2,1,0:T(8,128)S(1)}, bf16[4,32,128]{2,1,0:T(8,128)(2,1)S(1)}) custom-call(bf16[16,2,16,1024]{3,2,1,0:T(8,128)(2,1)S(1)} %all_to_all.10.pix_ref, s32[1,64]{1,0:T(1,128)S(1)} %get-tuple-element.15.look_ref, f32[1,128]{1,0:T(1,128)S(1)} %get-tuple-element.16.level_ref, s32[1,256]{1,0:T(1,128)S(1)} %get-tuple-element.17.half_ref, ...), custom_call_target="tpu_custom_call" | custom-call | tf_op jit(solution)/shard_map/phase_link/pallas_call | solution.py:376
  53.4 0.7 collective-permute-start.2
  54.1 0.0 collective-permute-done.2.edge_ref
  54.1 0.2 pack_rows.1
  54.4 20.2 %all_to_all.11.part_ref = bf16[16,48,128]{2,1,0:T(8,128)(2,1)S(1)} all-to-all(bf16[16,48,128]{2,1,0:T(8,128)(2,1)S(1)} %pack_rows.1), channel_id=1, replica_groups=mesh['date'=16,'az'=32] {'date'}, dimensions={0} | all-to-all | bytes 393216 | tf_op jit(solution)/shard_map/all_to_all | solution.py:409
  74.6 0.8 %overlap_add.1 = f32[2,2,128,128]{3,2,1,0:T(8,128)} custom-call(bf16[16,48,128]{2,1,0:T(8,128)(2,1)S(1)} %all_to_all.11.part_ref), custom_call_target="tpu_custom_call" | custom-call | tf_op jit(solution)/shard_map/overlap_add/pallas_call | solution.py:410
  (1 shorter events, 0.0 us)
Async XLA Ops:
  0.9 9.4 %collective-permute-start.1 = (bf16[2,2,16,128]{3,2,1,0:T(8,128)(2,1)S(1)}, bf16[2,2,16,128]{3,2,1,0:T(8,128)(2,1)S(1)}, u32[]{:S(2)}, u32[]{:S(2)}) collective-permute-start(bf16[2,2,16,128]{3,2,1,0:T(8,128)(2,1)S(1)} %get-tuple-element.23), channel_id=1, source_target_pairs={{1,2},{2,1},{3,4},{4,3},{5,6},{6,5},{7,8},{8,7},{9,10},{10,9},{11,... | collective-permute-start | bytes 49160 | tf_op jit(solution)/shard_map/ppermute | solution.py:329
  5.7 2.6 %copy-start = (f32[16,5]{0,1:T(8,128)S(1)}, f32[16,5]{0,1:T(8,128)}, u32[]{:S(2)}) copy-start(f32[16,5]{0,1:T(8,128)} %param.7) | copy-start | bytes 964
  5.7 4.6 %collective-permute-start = (bf16[2,2,16,128]{3,2,1,0:T(8,128)(2,1)S(1)}, bf16[2,2,16,128]{3,2,1,0:T(8,128)(2,1)S(1)}, u32[]{:S(2)}, u32[]{:S(2)}) collective-permute-start(bf16[2,2,16,128]{3,2,1,0:T(8,128)(2,1)S(1)} %get-tuple-element.24), channel_id=1, source_target_pairs={{0,1},{1,0},{2,3},{3,2},{4,5},{5,4},{6,7},{7,6},{8,9},{9,8},{10,11... | collective-permute-start | bytes 49160 | tf_op jit(solution)/shard_map/ppermute | solution.py:334
  53.4 0.7 collective-permute-start.2

commit v6 on v5

--- a/solution.py
+++ b/solution.py
@@ -128,15 +128,14 @@
 
 
 def link_kernel(
-    pix_ref, look_ref, level_ref, half_ref, basis_ref, stage_ref, edge_ref, proj
+    pix_ref, look_ref, level_ref, half_ref, basis_ref, gain_ref, edge_ref
 ):
     groups, _, dates_own, pixels = pix_ref.shape
     dates = groups * dates_own
     looks = look_ref.shape[1]
     width = 2 * looks
     bases = basis_ref.shape[0]
-    cols = stage_ref.shape[2]
-    block_rows = pixels // cols
+    cols = edge_ref.shape[2]
     place = lax.broadcasted_iota(jnp.int32, (pixels, width), 0)
     chosen = jnp.concatenate([look_ref[...], look_ref[...]], 1)
     picked = (place == chosen).astype(jnp.float32).astype(jnp.bfloat16)
@@ -202,19 +201,50 @@
     right = gain[:, dates:]
     gain_re = jnp.concatenate([left, -right], 0).astype(jnp.bfloat16)
     gain_im = jnp.concatenate([right, left], 0).astype(jnp.bfloat16)
-    proj[...] = dot(gain_re, pix_ref[:, 0].reshape(dates, pixels)) + dot(
-        gain_im, pix_ref[:, 1].reshape(dates, pixels)
-    )
-
+    gain_ref[:, :dates] = gain_re
+    gain_ref[:, dates:] = gain_im
+
+    opens = lax.axis_index("date") == 0
+    side = pl.multiple_of(jnp.where(opens, 0, pixels - REACH * cols), cols)
+    outer = [
+        pix_ref[:, c, :, pl.ds(side, REACH * cols)].reshape(dates, REACH * cols)
+        for c in range(2)
+    ]
+    rows = (REACH + 1) * bases
+    tops, bottoms = {}, {}
+    for c in range(2):
+        lines = slice(c * rows + bases, (c + 1) * rows)
+        proj = dot(gain_re[lines], outer[0]) + dot(gain_im[lines], outer[1])
+
+        def part(j, row):
+            return proj[(j - 1) * bases : j * bases, row * cols : (row + 1) * cols]
+
+        above = [part(2, 0), part(1, 0) + part(2, 1)]
+        below = [part(2, 0) + part(1, 1), part(2, 1)]
+        tops[c] = above
+        bottoms[c] = below
+    up = tops[1] + tops[0]
+    down = bottoms[0] + bottoms[1]
+    for i in range(2 * REACH):
+        edge_ref[i] = jnp.where(opens, up[i], down[i]).astype(jnp.bfloat16)
+
+
+def project_kernel(pix_ref, gain_ref, out_ref, lent_ref, proj, stage):
+    groups, _, dates_own, pixels = pix_ref.shape
+    dates = groups * dates_own
+    bases, cols = lent_ref.shape[1:]
+    block_rows = pixels // cols
+    proj[...] = dot(gain_ref[:, :dates], pix_ref[:, 0].reshape(dates, pixels)) + dot(
+        gain_ref[:, dates:], pix_ref[:, 1].reshape(dates, pixels)
+    )
     below = [block_rows, block_rows + 1]
     above = [-2, -1]
     slots = [(0, r) for r in range(block_rows)] + [(1, r) for r in range(block_rows)]
     slots += [(0, r) for r in below] + [(1, r) for r in below]
     slots += [(1, r) for r in above] + [(0, r) for r in above]
+    inner = 2 * block_rows
     sub = 8
-    opens = lax.axis_index("date") == 0
     for k in range(0, bases, sub):
-        rest = {}
         for c in range(2):
             terms = [
                 [
@@ -234,39 +264,39 @@
                     if 0 <= row + j < block_rows:
                         term = terms[abs(j)][row + j]
                         out = term if out is None else out + term
-                stage_ref[q, pl.ds(k, sub), :] = out
-                rest[q] = out
-        base = 2 * block_rows
-        for i in range(2 * REACH):
-            edge = jnp.where(opens, rest[base + 2 * REACH + i], rest[base + i])
-            edge_ref[i, pl.ds(k, sub), :] = edge.astype(jnp.bfloat16)
-
-
-def pack_kernel(stage_ref, edge_ref, out_ref, held):
-    groups = out_ref.shape[0]
-    slots, bases, _ = stage_ref.shape
-    sub = slots // 3
+                if q < inner:
+                    stage[pl.ds(q * bases + k, sub), :] = out
+                else:
+                    lent_ref[q - inner, pl.ds(k, sub), :] = out
+    own = bases // groups
+    for d in range(groups):
+        rows = [
+            stage[pl.ds(c * block_rows * bases + d * own + k, block_rows, stride=bases), :]
+            for k in range(own)
+            for c in range(2)
+        ]
+        out_ref[d, : len(rows) * block_rows, :] = jnp.concatenate(rows, 0).astype(
+            jnp.bfloat16
+        )
+
+
+def pack_kernel(part_ref, lent_ref, edge_ref, out_ref, held):
+    del part_ref
+    groups, height, _ = out_ref.shape
+    slots, bases, _ = lent_ref.shape
     own = bases // groups
     opens = lax.axis_index("date") == 0
     closes = lax.axis_index("date") == groups - 1
-    for q in range(slots):
-        value = stage_ref[q]
-        i = q - 2 * sub
+    for i in range(slots):
+        value = lent_ref[i]
         if i >= 2 * REACH:
             value = jnp.where(opens, edge_ref[i - 2 * REACH].astype(jnp.float32), value)
-        elif i >= 0:
+        else:
             value = jnp.where(closes, edge_ref[i].astype(jnp.float32), value)
-        held[pl.ds(q * bases, bases), :] = value
+        held[pl.ds(i * bases, bases), :] = value
     for d in range(groups):
-        lines = [
-            [
-                held[pl.ds(q * sub * bases + d * own + k, sub, stride=bases), :]
-                for q in range(3)
-            ]
-            for k in range(own)
-        ]
-        rows = [v for k in range(own) for v in lines[k][:2]] + [lines[k][2] for k in range(own)]
-        out_ref[d] = jnp.concatenate(rows, 0).astype(jnp.bfloat16)
+        rows = [held[pl.ds(d * own + k, slots, stride=bases), :] for k in range(own)]
+        out_ref[d, height - own * slots :, :] = jnp.concatenate(rows, 0).astype(jnp.bfloat16)
 
 
 def join_kernel(part_ref, out_ref):
@@ -372,40 +402,51 @@
     )(on_chip(blocks), on_chip(rim), on_chip(near), on_chip(far), on_chip(taps))
     pix = lax.all_to_all(blocks, "date", split_axis=0, concat_axis=0, tiled=True)
 
-    slots = 3 * block_rows
-    stage, edge = pl.pallas_call(
+    pix = on_chip(pix)
+    rows_all = 2 * (REACH + 1) * bases
+    gain, edge = pl.pallas_call(
         link_kernel,
         out_shape=(
-            chip_out((slots, bases, cols), jnp.float32),
+            chip_out((rows_all, 2 * dates), jnp.bfloat16),
             chip_out((2 * REACH, bases, cols), jnp.bfloat16),
         ),
         in_specs=[VMEM] * 5,
         out_specs=(VMEM, VMEM),
-        scratch_shapes=[pltpu.VMEM((2 * (REACH + 1) * bases, pixels), jnp.float32)],
         interpret=INTERPRET,
         name="phase_link",
-    )(
-        on_chip(pix),
-        on_chip(look),
-        on_chip(level),
-        on_chip(half),
-        on_chip(basis),
-    )
+    )(pix, on_chip(look), on_chip(level), on_chip(half), on_chip(basis))
     edge = lax.ppermute(
         edge,
         ("date", "az"),
         [((groups - 1) * slabs + a, (groups - 1) * slabs + a + 1) for a in range(slabs - 1)]
         + [(a + 1, a) for a in range(slabs - 1)],
     )
+    packed = (groups, 3 * own * block_rows, cols)
+    own_rows, lent = pl.pallas_call(
+        project_kernel,
+        out_shape=(
+            chip_out(packed, jnp.bfloat16),
+            chip_out((4 * REACH, bases, cols), jnp.float32),
+        ),
+        in_specs=[VMEM, VMEM],
+        out_specs=(VMEM, VMEM),
+        scratch_shapes=[
+            pltpu.VMEM((rows_all, pixels), jnp.float32),
+            pltpu.VMEM((2 * block_rows * bases, cols), jnp.float32),
+        ],
+        interpret=INTERPRET,
+        name="project",
+    )(pix, on_chip(gain))
     lent = pl.pallas_call(
         pack_kernel,
-        out_shape=chip_out((groups, 3 * own * block_rows, cols), jnp.bfloat16),
-        in_specs=[VMEM, VMEM],
+        out_shape=chip_out(packed, jnp.bfloat16),
+        in_specs=[VMEM] * 3,
         out_specs=VMEM,
-        scratch_shapes=[pltpu.VMEM((slots * bases, cols), jnp.float32)],
+        scratch_shapes=[pltpu.VMEM((4 * REACH * bases, cols), jnp.float32)],
+        input_output_aliases={0: 0},
         interpret=INTERPRET,
         name="pack_rows",
-    )(on_chip(stage), on_chip(edge))
+    )(on_chip(own_rows), on_chip(lent), on_chip(edge))
     parts = lax.all_to_all(lent, "date", split_axis=0, concat_axis=0, tiled=True)
     return pl.pallas_call(
         join_kernel,

time: 75.7 us -> 75.4 us (level)
    pallas_call x2 -> x3, Pallas kernels: 3.17 us -> 3.39 us  [the longest x1 2.76 us: on_device(): pl.pallas_call(link_kernel, out_shape=(chip_out((rows_all, 2 * dates), jn...]
where the time goes in v6:
time: 75.4 us; the launch traced here: 75.1 us
  blocking collectives  59.7 us (79%)
  starting transfers between devices  7.36 us (10%)
  Pallas kernels  6.29 us (8%)
  local copies, waits for them, and re-layouts  0.91 us (1%)
  between operations  0.76 us (1%)
    all_to_all x1, blocking collectives, on_device(): lax.all_to_all(blocks, 'date', split_axis=0, concat_axis=0, tiled=True)  40 us
    all_to_all x1, blocking collectives, on_device(): lax.all_to_all(lent, 'date', split_axis=0, concat_axis=0, tiled=True)  19.7 us
    ppermute x1, starting transfers between devices, on_device(): lax.ppermute(jnp.where(odd == 0, start, last), 'az', swaps([(i, i + 1) fo...  4.78 us
    pallas_call x1, Pallas kernels, on_device(): pl.pallas_call(link_kernel, out_shape=(chip_out((rows_all, 2 * dates), jn...  2.76 us
    pallas_call x1, Pallas kernels, on_device(): pl.pallas_call(filter_kernel, out_shape=(chip_out(shape, jnp.bfloat16), c...  1.98 us
    ppermute x1, starting transfers between devices, on_device(): lax.ppermute(jnp.where(odd == 0, last, start), 'az', swaps([(i, i + 1) fo...  1.92 us
  transfers between devices with their start and end apart: 3, of which 0 were waited for; matrix products, arithmetic and copies ran while one was open for 0% of the time, Pallas kernels for 3%

profile of v6, /device:TPU:40, one launch (start us, length us, event | category | flops | bytes accessed | tf_op | source)
XLA Modules:
  0.0 75.1 jit_solution(15766496807216508541)
XLA Ops:
  0.0 0.9 %fusion = (bf16[2,16,2,128]{3,2,1,0:T(2,128)(2,1)S(1)}, bf16[2,16,2,128]{3,2,1,0:T(2,128)(2,1)S(1)}) fusion(bf16[2,16,128,128]{3,2,1,0:T(8,128)(2,1)} %slc_hbm.1), kind=kLoop, calls=%fused_computation.2 | loop fusion | bytes 65536 | tf_op jit(solution)/shard_map/slice | solution.py:357
  0.9 4.8 %collective-permute-start.1 = (bf16[2,2,16,128]{3,2,1,0:T(8,128)(2,1)S(1)}, bf16[2,2,16,128]{3,2,1,0:T(8,128)(2,1)S(1)}, u32[]{:S(2)}, u32[]{:S(2)}) collective-permute-start(bf16[2,2,16,128]{3,2,1,0:T(8,128)(2,1)S(1)} %get-tuple-element.27), channel_id=1, source_target_pairs={{1,2},{2,1},{3,4},{4,3},{5,6},{6,5},{7,8},{8,7},{9,10},{10,9},{11,... | collective-permute-start | bytes 49160 | tf_op jit(solution)/shard_map/ppermute | solution.py:359
  5.7 0.0 copy-start
  5.7 1.9 %collective-permute-start = (bf16[2,2,16,128]{3,2,1,0:T(8,128)(2,1)S(1)}, bf16[2,2,16,128]{3,2,1,0:T(8,128)(2,1)S(1)}, u32[]{:S(2)}, u32[]{:S(2)}) collective-permute-start(bf16[2,2,16,128]{3,2,1,0:T(8,128)(2,1)S(1)} %get-tuple-element.28), channel_id=1, source_target_pairs={{0,1},{1,0},{2,3},{3,2},{4,5},{5,4},{6,7},{7,6},{8,9},{9,8},{10,11... | collective-permute-start | bytes 49160 | tf_op jit(solution)/shard_map/ppermute | solution.py:364
  8.3 0.0 copy-done
  8.3 2.0 %azimuth_filter.1 = (bf16[16,2,16,1024]{3,2,1,0:T(8,128)(2,1)S(1)}, f32[2,2,4,16,128]{4,3,2,1,0:T(8,128)S(1)}, s32[1,64]{1,0:T(1,128)S(1)}, f32[1,128]{1,0:T(1,1...) custom-call(bf16[2,16,128,128]{3,2,1,0:T(8,128)(2,1)} %slc_hbm.1, f32[5,16]{1,0:T(8,128)S(1)} %bitcast.7, ...), custom_call_target="tpu_custom_call" | custom-call | tf_op jit(solution)/shard_map/azimuth_filter/pallas_call | solution.py:374
  10.3 0.0 collective-permute-done.1.far_ref
  10.3 0.0 collective-permute-done.near_ref
  10.3 0.2 filter_rim.1
  10.5 40.0 %all_to_all.10.pix_ref = bf16[16,2,16,1024]{3,2,1,0:T(8,128)(2,1)S(1)} all-to-all(bf16[16,2,16,1024]{3,2,1,0:T(8,128)(2,1)S(1)} %filter_rim.1), channel_id=1, replica_groups=mesh['date'=16,'az'=32] {'date'}, dimensions={0} | all-to-all | bytes 2097152 | tf_op jit(solution)/shard_map/all_to_all | solution.py:403
  50.5 2.8 %phase_link.1 = (bf16[192,512]{1,0:T(8,128)(2,1)S(1)}, bf16[4,32,128]{2,1,0:T(8,128)(2,1)S(1)}) custom-call(bf16[16,2,16,1024]{3,2,1,0:T(8,128)(2,1)S(1)} %all_to_all.10.pix_ref, s32[1,64]{1,0:T(1,128)S(1)} %get-tuple-element.17.look_ref, f32[1,128]{1,0:T(1,128)S(1)} %get-tuple-element.18.level_ref, s32[1,256]{1,0:T(1,128)S(1)} %get-tuple-element.19.half_ref, ...), custom_call_target="tpu_custom_call" | custom-call | tf_op jit(solution)/shard_map/phase_link/pallas_call | solution.py:407
  53.3 0.7 collective-permute-start.2
  54.0 0.5 project.1
  54.5 0.0 collective-permute-done.2.edge_ref
  54.5 0.1 pack_rows.1
  54.6 19.7 %all_to_all.11.part_ref = bf16[16,48,128]{2,1,0:T(8,128)(2,1)S(1)} all-to-all(bf16[16,48,128]{2,1,0:T(8,128)(2,1)S(1)} %pack_rows.1), channel_id=1, replica_groups=mesh['date'=16,'az'=32] {'date'}, dimensions={0} | all-to-all | bytes 393216 | tf_op jit(solution)/shard_map/all_to_all | solution.py:450
  74.3 0.8 %overlap_add.1 = f32[2,2,128,128]{3,2,1,0:T(8,128)} custom-call(bf16[16,48,128]{2,1,0:T(8,128)(2,1)S(1)} %all_to_all.11.part_ref), custom_call_target="tpu_custom_call" | custom-call | tf_op jit(solution)/shard_map/overlap_add/pallas_call | solution.py:451
  (1 shorter events, 0.0 us)
Async XLA Ops:
  0.9 9.4 %collective-permute-start.1 = (bf16[2,2,16,128]{3,2,1,0:T(8,128)(2,1)S(1)}, bf16[2,2,16,128]{3,2,1,0:T(8,128)(2,1)S(1)}, u32[]{:S(2)}, u32[]{:S(2)}) collective-permute-start(bf16[2,2,16,128]{3,2,1,0:T(8,128)(2,1)S(1)} %get-tuple-element.27), channel_id=1, source_target_pairs={{1,2},{2,1},{3,4},{4,3},{5,6},{6,5},{7,8},{8,7},{9,10},{10,9},{11,... | collective-permute-start | bytes 49160 | tf_op jit(solution)/shard_map/ppermute | solution.py:359
  5.7 2.6 %copy-start = (f32[16,5]{0,1:T(8,128)S(1)}, f32[16,5]{0,1:T(8,128)}, u32[]{:S(2)}) copy-start(f32[16,5]{0,1:T(8,128)} %param.7) | copy-start | bytes 964
  5.7 4.6 %collective-permute-start = (bf16[2,2,16,128]{3,2,1,0:T(8,128)(2,1)S(1)}, bf16[2,2,16,128]{3,2,1,0:T(8,128)(2,1)S(1)}, u32[]{:S(2)}, u32[]{:S(2)}) collective-permute-start(bf16[2,2,16,128]{3,2,1,0:T(8,128)(2,1)S(1)} %get-tuple-element.28), channel_id=1, source_target_pairs={{0,1},{1,0},{2,3},{3,2},{4,5},{5,4},{6,7},{7,6},{8,9},{9,8},{10,11... | collective-permute-start | bytes 49160 | tf_op jit(solution)/shard_map/ppermute | solution.py:364
  53.3 1.2 %collective-permute-start.2 = (bf16[4,32,128]{2,1,0:T(8,128)(2,1)S(1)}, bf16[4,32,128]{2,1,0:T(8,128)(2,1)S(1)}, u32[]{:S(2)}, u32[]{:S(2)}) collective-permute-start(bf16[4,32,128]{2,1,0:T(8,128)(2,1)S(1)} %get-tuple-element.24), channel_id=1, source_target_pairs={{480,481},{481,482},{482,483},{483,484},{484,485},{485,486},{486,4... | collective-permute-start | bytes 98312 | tf_op jit(solution)/shard_map/ppermute | solution.py:418

commit v7 on v6

--- a/solution.py
+++ b/solution.py
@@ -26,44 +26,74 @@
     return total.astype(jnp.bfloat16)
 
 
-def filter_kernel(
+def fetch_kernel(
     slc_hbm,
-    taps_ref,
+    taps_hbm,
     look_hbm,
-    level_smem,
     half_hbm,
     basis_hbm,
-    out_ref,
-    rim_ref,
+    slc_ref,
+    near_ref,
+    far_ref,
+    taps_ref,
     look_ref,
-    level_ref,
     half_ref,
     basis_ref,
-    slc_ref,
     held,
     sems,
 ):
+    _, dates, rows, _ = slc_ref.shape
+    tile = held.shape[0] // dates
+    spans = [(0, tile), (rows - tile, tile), (tile, rows - 2 * tile)]
+    loads = [
+        pltpu.make_async_copy(
+            slc_hbm.at[:, :, pl.ds(start, size), :],
+            slc_ref.at[:, :, pl.ds(start, size), :],
+            sems.at[i],
+        )
+        for i, (start, size) in enumerate(spans)
+    ]
+    small = [
+        (taps_hbm, taps_ref),
+        (look_hbm, look_ref),
+        (half_hbm, half_ref),
+        (basis_hbm, basis_ref),
+    ]
+    loads += [
+        pltpu.make_async_copy(a, b, sems.at[len(spans) + i])
+        for i, (a, b) in enumerate(small)
+    ]
+    for load in loads:
+        load.start()
+    even = (lax.axis_index("az") & 1) == 0
+    loads[0].wait()
+    loads[1].wait()
+    for c in range(2):
+        edges = []
+        for start, row in ((0, 0), (rows - tile, tile - REACH)):
+            for t in range(dates):
+                held[pl.ds(t * tile, tile), :] = slc_ref[
+                    c, t, pl.ds(start, tile), :
+                ].astype(jnp.float32)
+            edges.append(
+                [held[pl.ds(row + i, dates, stride=tile), :] for i in range(REACH)]
+            )
+        for i in range(REACH):
+            first, last = edges[0][i], edges[1][i]
+            near_ref[c, i] = jnp.where(even, last, first).astype(jnp.bfloat16)
+            far_ref[c, i] = jnp.where(even, first, last).astype(jnp.bfloat16)
+    for load in loads[2:]:
+        load.wait()
+
+
+def filter_kernel(slc_ref, taps_ref, level_smem, out_ref, rim_ref, level_ref, held):
     _, dates, rows, cols = slc_ref.shape
     blocks = out_ref.shape[0]
     block_rows = rows // blocks
     pitch = held.shape[0] // dates
     taps = spread(taps_ref, cols)
-    loads = [
-        pltpu.make_async_copy(slc_hbm.at[c], slc_ref.at[c], sems.at[c]) for c in range(2)
-    ]
-    small = [
-        (look_hbm, look_ref),
-        (half_hbm, half_ref),
-        (basis_hbm, basis_ref),
-    ]
-    copies = [
-        pltpu.make_async_copy(a, b, sems.at[2 + i]) for i, (a, b) in enumerate(small)
-    ]
-    for copy in loads + copies:
-        copy.start()
     level_ref[...] = jnp.full(level_ref.shape, level_smem[0, 0].astype(jnp.float32))
     for c in range(2):
-        loads[c].wait()
         for t in range(dates):
             held[pl.ds(t * pitch, rows), :] = slc_ref[c, t].astype(jnp.float32)
 
@@ -80,8 +110,6 @@
             window.pop(0)
         for i in range(2 * REACH):
             rim_ref[1, c, i] = window[i]
-    for copy in copies:
-        copy.wait()
 
 
 def rim_kernel(part_ref, rim_ref, near_ref, far_ref, taps_ref, out_ref):
@@ -178,9 +206,10 @@
     t = scale * alpha
     x = jnp.ones_like(t)
     w = (scale * beta) * inner
-    m = (2.0 - 2.0 * t) * identity - w
-    u = -identity
-    w = (2.0 - 2.0 * t) * w - dot3(w, whole(w))
+    full = whole(w)
+    m = (2.0 - 2.0 * t) * seen - dot3(seen, full)
+    u = -seen
+    w = (2.0 - 2.0 * t) * w - dot3(w, full)
     x, t = x * (2.0 - t), 2.0 * t - t * t
     for step in range(1, NS_ITERS):
         full = whole(w)
@@ -188,12 +217,12 @@
             w = (2.0 - 2.0 * t) * w - dot3(w, full)
         prod = dot3(jnp.concatenate([m, u], 0), full)
         m, u = (
-            (2.0 - 2.0 * t) * m - prod[:looks],
-            (2.0 - t) * u - x * m - prod[looks:],
+            (2.0 - 2.0 * t) * m - prod[: m.shape[0]],
+            (2.0 - t) * u - x * m - prod[m.shape[0] :],
         )
         x, t = x * (2.0 - t), 2.0 * t - t * t
 
-    core = dot3(seen, whole((scale * beta) * (m - (mean * scale) * u)))
+    core = (scale * beta) * (m - (mean * scale) * u)
     core_hi, core_lo = split(core)
     gain = dot(core_hi, wide) + dot(core_lo, wide)
     plain = (t - mean * scale * x) * near
@@ -353,44 +382,42 @@
     bases, dates = basis.shape
     own = bases // groups
 
-    odd = lax.axis_index("az") & 1
-    last = jnp.swapaxes(slc_stack[:, :, rows - REACH :, :], 1, 2)
-    start = jnp.swapaxes(slc_stack[:, :, :REACH, :], 1, 2)
-    far = lax.ppermute(
-        jnp.where(odd == 0, start, last),
-        "az",
-        swaps([(i, i + 1) for i in range(1, slabs - 1, 2)]),
-    )
-    near = lax.ppermute(
-        jnp.where(odd == 0, last, start),
-        "az",
-        swaps([(i, i + 1) for i in range(0, slabs - 1, 2)]),
-    )
+    rim_shape = (2, REACH, date_local, cols)
+    small = (fir_taps.T, look_index.reshape(1, -1), window_half.reshape(1, dates), basis)
+    fetched, near, far, taps, look, half, basis = pl.pallas_call(
+        fetch_kernel,
+        out_shape=(
+            chip_out(slc_stack.shape, jnp.bfloat16),
+            chip_out(rim_shape, jnp.bfloat16),
+            chip_out(rim_shape, jnp.bfloat16),
+        )
+        + tuple(chip_out(x.shape, x.dtype) for x in small),
+        in_specs=[ANY] * 5,
+        out_specs=(VMEM,) * 7,
+        scratch_shapes=[
+            pltpu.VMEM((date_local * 16, cols), jnp.float32),
+            pltpu.SemaphoreType.DMA((7,)),
+        ],
+        interpret=INTERPRET,
+        name="fetch",
+    )(slc_stack, *small)
+    near = lax.ppermute(near, "az", swaps([(i, i + 1) for i in range(0, slabs - 1, 2)]))
+    far = lax.ppermute(far, "az", swaps([(i, i + 1) for i in range(1, slabs - 1, 2)]))
     pitch = rows + 8
     shape = (groups, 2, date_local, pixels)
-    look = look_index.reshape(1, -1)
-    half = window_half.reshape(1, dates)
-    taps = fir_taps.T
-    blocks, rim, look, level, half, basis = pl.pallas_call(
+    blocks, rim, level = pl.pallas_call(
         filter_kernel,
         out_shape=(
             chip_out(shape, jnp.bfloat16),
             chip_out((2, 2, 2 * REACH, date_local, cols), jnp.float32),
-            chip_out(look.shape, look.dtype),
             chip_out((1, cols), jnp.float32),
-            chip_out(half.shape, half.dtype),
-            chip_out(basis.shape, basis.dtype),
         ),
-        in_specs=[ANY, VMEM, ANY, SMEM, ANY, ANY],
-        out_specs=(VMEM,) * 6,
-        scratch_shapes=[
-            pltpu.VMEM(slc_stack.shape, jnp.bfloat16),
-            pltpu.VMEM((date_local * pitch, cols), jnp.float32),
-            pltpu.SemaphoreType.DMA((5,)),
-        ],
+        in_specs=[VMEM, VMEM, SMEM],
+        out_specs=(VMEM,) * 3,
+        scratch_shapes=[pltpu.VMEM((date_local * pitch, cols), jnp.float32)],
         interpret=INTERPRET,
         name="azimuth_filter",
-    )(slc_stack, on_chip(taps), look, shrink_level, half, basis)
+    )(on_chip(fetched), on_chip(taps), shrink_level)
     blocks = pl.pallas_call(
         rim_kernel,
         out_shape=chip_out(shape, jnp.bfloat16),

time: 75.4 us -> 72.4 us (0.960)
  blocking collectives: 59.7 us -> 54.8 us
  waiting for transfers between devices: 0.01 us -> 2.23 us
  local copies, waits for them, and re-layouts: 0.91 us -> 0 us
    all_to_all x1, blocking collectives: 40 us -> 35.8 us  [on_device(): lax.all_to_all(blocks, 'date', split_axis=0, concat_axis=0, tiled=True)]
    ppermute x2, waiting for transfers between devices: 0.01 us -> 2.23 us  [the longest x1 2.23 us: on_device(): lax.ppermute(far, 'az', swaps([(i, i + 1) for i in range(1, slabs - 1, 2)]))]
    pallas_call x0 -> x1, Pallas kernels: none -> 1.34 us  [on_device(): pl.pallas_call(fetch_kernel, out_shape=(chip_out(slc_stack.shape, jnp.bfl...]
    pallas_call x1, Pallas kernels: 1.98 us -> 0.93 us  [on_device(): pl.pallas_call(filter_kernel, out_shape=(chip_out(shape, jnp.bfloat16), c...]
    slice x1 -> x0, local copies, waits for them, and re-layouts: 0.9 us -> none  [on_device(): last = jnp.swapaxes(slc_stack[:, :, rows - REACH:, :], 1, 2)]
  transfers between devices with their start and end apart: 3 -> 3, of which waited for: 0 -> 1; matrix products, arithmetic and copies ran while one was open for 0% -> 0% of each run, Pallas kernels for 3% -> 2%
where the time goes in v7:
time: 72.4 us; the launch traced here: 72.2 us
  blocking collectives  54.8 us (76%)
  starting transfers between devices  8.02 us (11%)
  Pallas kernels  6.42 us (9%)
  waiting for transfers between devices  2.23 us (3%)
  between operations  0.73 us (1%)
    all_to_all x1, blocking collectives, on_device(): lax.all_to_all(blocks, 'date', split_axis=0, concat_axis=0, tiled=True)  35.8 us
    all_to_all x1, blocking collectives, on_device(): lax.all_to_all(lent, 'date', split_axis=0, concat_axis=0, tiled=True)  18.9 us
    ppermute x1, starting transfers between devices, on_device(): lax.ppermute(far, 'az', swaps([(i, i + 1) for i in range(1, slabs - 1, 2)]))  5.44 us
    pallas_call x1, Pallas kernels, on_device(): pl.pallas_call(link_kernel, out_shape=(chip_out((rows_all, 2 * dates), jn...  2.6 us
    ppermute x1, waiting for transfers between devices, on_device(): lax.ppermute(far, 'az', swaps([(i, i + 1) for i in range(1, slabs - 1, 2)]))  2.23 us
    ppermute x1, starting transfers between devices, on_device(): lax.ppermute(near, 'az', swaps([(i, i + 1) for i in range(0, slabs - 1, 2...  1.92 us
  transfers between devices with their start and end apart: 3, of which 1 were waited for; matrix products, arithmetic and copies ran while one was open for 0% of the time, Pallas kernels for 2%

profile of v7, /device:TPU:40, one launch (start us, length us, event | category | flops | bytes accessed | tf_op | source)
XLA Modules:
  0.0 72.2 jit_solution(18217136544069322363)
XLA Ops:
  0.0 1.3 %fetch.1 = (bf16[2,16,128,128]{3,2,1,0:T(8,128)(2,1)S(1)}, bf16[2,2,16,128]{3,2,1,0:T(8,128)(2,1)S(1)}, bf16[2,2,16,128]{3,2,1,0:T(8,128)(2,1)S(1)}, f32[5,16]{1...) custom-call(bf16[2,16,128,128]{3,2,1,0:T(8,128)(2,1)} %slc_hbm.1, ...), custom_call_target="tpu_custom_call" | custom-call | tf_op jit(solution)/shard_map/fetch/pallas_call | solution.py:387
  1.4 1.9 %collective-permute-start = (bf16[2,2,16,128]{3,2,1,0:T(8,128)(2,1)S(1)}, bf16[2,2,16,128]{3,2,1,0:T(8,128)(2,1)S(1)}, u32[]{:S(2)}, u32[]{:S(2)}) collective-permute-start(bf16[2,2,16,128]{3,2,1,0:T(8,128)(2,1)S(1)} %get-tuple-element.23), channel_id=1, source_target_pairs={{0,1},{1,0},{2,3},{3,2},{4,5},{5,4},{6,7},{7,6},{8,9},{9,8},{10,11... | collective-permute-start | bytes 49160 | tf_op jit(solution)/shard_map/ppermute | solution.py:404
  3.3 5.4 %collective-permute-start.1 = (bf16[2,2,16,128]{3,2,1,0:T(8,128)(2,1)S(1)}, bf16[2,2,16,128]{3,2,1,0:T(8,128)(2,1)S(1)}, u32[]{:S(2)}, u32[]{:S(2)}) collective-permute-start(bf16[2,2,16,128]{3,2,1,0:T(8,128)(2,1)S(1)} %get-tuple-element.24), channel_id=1, source_target_pairs={{1,2},{2,1},{3,4},{4,3},{5,6},{6,5},{7,8},{8,7},{9,10},{10,9},{11,... | collective-permute-start | bytes 49160 | tf_op jit(solution)/shard_map/ppermute | solution.py:405
  9.4 0.9 %azimuth_filter.1 = (bf16[16,2,16,1024]{3,2,1,0:T(8,128)(2,1)S(1)}, f32[2,2,4,16,128]{4,3,2,1,0:T(8,128)S(1)}, f32[1,128]{1,0:T(1,128)S(1)}) custom-call(bf16[2,16,128,128]{3,2,1,0:T(8,128)(2,1)S(1)} %get-tuple-element.19.slc_ref, f32[5,16]{1,0:T(8,128)S(1)} %get-tuple-element.20.taps_ref, s32[1,1]{1,0:T(1,128)S(6)} %copy.11.level_smem), custom_call_target="tpu_custom_call" | custom-call | tf_op jit(solution)/shard_map/azimuth_filter/pallas_call | solution.py:408
  10.3 0.0 collective-permute-done.near_ref
  10.3 2.2 %collective-permute-done.1.far_ref = bf16[2,2,16,128]{3,2,1,0:T(8,128)(2,1)S(1)} collective-permute-done((bf16[2,2,16,128]{3,2,1,0:T(8,128)(2,1)S(1)}, bf16[2,2,16,128]{3,2,1,0:T(8,128)(2,1)S(1)}, u32[]{:S(2)}, u32[]{:S(2)}) %collective-permute-start.1) | collective-permute-done | bytes 16416 | tf_op jit(solution)/shard_map/ppermute | solution.py:405
  12.6 0.2 filter_rim.1
  12.7 35.8 %all_to_all.10.pix_ref = bf16[16,2,16,1024]{3,2,1,0:T(8,128)(2,1)S(1)} all-to-all(bf16[16,2,16,1024]{3,2,1,0:T(8,128)(2,1)S(1)} %filter_rim.1), channel_id=1, replica_groups=mesh['date'=16,'az'=32] {'date'}, dimensions={0} | all-to-all | bytes 2097152 | tf_op jit(solution)/shard_map/all_to_all | solution.py:430
  48.6 2.6 %phase_link.1 = (bf16[192,512]{1,0:T(8,128)(2,1)S(1)}, bf16[4,32,128]{2,1,0:T(8,128)(2,1)S(1)}) custom-call(bf16[16,2,16,1024]{3,2,1,0:T(8,128)(2,1)S(1)} %all_to_all.10.pix_ref, s32[1,64]{1,0:T(1,128)S(1)} %get-tuple-element.25.look_ref, f32[1,128]{1,0:T(1,128)S(1)} %get-tuple-element.26.level_ref, s32[1,256]{1,0:T(1,128)S(1)} %get-tuple-element.27.half_ref, ...), custom_call_target="tpu_custom_call" | custom-call | tf_op jit(solution)/shard_map/phase_link/pallas_call | solution.py:434
  51.2 0.7 collective-permute-start.2
  51.9 0.5 project.1
  52.4 0.0 collective-permute-done.2.edge_ref
  52.4 0.1 pack_rows.1
  52.5 18.9 %all_to_all.11.part_ref = bf16[16,48,128]{2,1,0:T(8,128)(2,1)S(1)} all-to-all(bf16[16,48,128]{2,1,0:T(8,128)(2,1)S(1)} %pack_rows.1), channel_id=1, replica_groups=mesh['date'=16,'az'=32] {'date'}, dimensions={0} | all-to-all | bytes 393216 | tf_op jit(solution)/shard_map/all_to_all | solution.py:477
  71.4 0.8 %overlap_add.1 = f32[2,2,128,128]{3,2,1,0:T(8,128)} custom-call(bf16[16,48,128]{2,1,0:T(8,128)(2,1)S(1)} %all_to_all.11.part_ref), custom_call_target="tpu_custom_call" | custom-call | tf_op jit(solution)/shard_map/overlap_add/pallas_call | solution.py:478
Async XLA Ops:
  1.4 9.0 %collective-permute-start = (bf16[2,2,16,128]{3,2,1,0:T(8,128)(2,1)S(1)}, bf16[2,2,16,128]{3,2,1,0:T(8,128)(2,1)S(1)}, u32[]{:S(2)}, u32[]{:S(2)}) collective-permute-start(bf16[2,2,16,128]{3,2,1,0:T(8,128)(2,1)S(1)} %get-tuple-element.23), channel_id=1, source_target_pairs={{0,1},{1,0},{2,3},{3,2},{4,5},{5,4},{6,7},{7,6},{8,9},{9,8},{10,11... | collective-permute-start | bytes 49160 | tf_op jit(solution)/shard_map/ppermute | solution.py:404
  3.3 9.3 %collective-permute-start.1 = (bf16[2,2,16,128]{3,2,1,0:T(8,128)(2,1)S(1)}, bf16[2,2,16,128]{3,2,1,0:T(8,128)(2,1)S(1)}, u32[]{:S(2)}, u32[]{:S(2)}) collective-permute-start(bf16[2,2,16,128]{3,2,1,0:T(8,128)(2,1)S(1)} %get-tuple-element.24), channel_id=1, source_target_pairs={{1,2},{2,1},{3,4},{4,3},{5,6},{6,5},{7,8},{8,7},{9,10},{10,9},{11,... | collective-permute-start | bytes 49160 | tf_op jit(solution)/shard_map/ppermute | solution.py:405
  51.2 1.2 %collective-permute-start.2 = (bf16[4,32,128]{2,1,0:T(8,128)(2,1)S(1)}, bf16[4,32,128]{2,1,0:T(8,128)(2,1)S(1)}, u32[]{:S(2)}, u32[]{:S(2)}) collective-permute-start(bf16[4,32,128]{2,1,0:T(8,128)(2,1)S(1)} %get-tuple-element.32), channel_id=1, source_target_pairs={{480,481},{481,482},{482,483},{483,484},{484,485},{485,486},{486,4... | collective-permute-start | bytes 98312 | tf_op jit(solution)/shard_map/ppermute | solution.py:445

commit v8 on v7

--- a/solution.py
+++ b/solution.py
@@ -44,14 +44,22 @@
 ):
     _, dates, rows, _ = slc_ref.shape
     tile = held.shape[0] // dates
-    spans = [(0, tile), (rows - tile, tile), (tile, rows - 2 * tile)]
+    parts = 4
+    share = dates // parts
+    spans = [(pl.ds(0, 2), pl.ds(0, dates), 0, tile)]
+    spans += [(pl.ds(0, 2), pl.ds(0, dates), rows - tile, tile)]
+    spans += [
+        (pl.ds(c, 1), pl.ds(i * share, share), tile, rows - 2 * tile)
+        for c in range(2)
+        for i in range(parts)
+    ]
     loads = [
         pltpu.make_async_copy(
-            slc_hbm.at[:, :, pl.ds(start, size), :],
-            slc_ref.at[:, :, pl.ds(start, size), :],
+            slc_hbm.at[c, t, pl.ds(start, size), :],
+            slc_ref.at[c, t, pl.ds(start, size), :],
             sems.at[i],
         )
-        for i, (start, size) in enumerate(spans)
+        for i, (c, t, start, size) in enumerate(spans)
     ]
     small = [
         (taps_hbm, taps_ref),
@@ -173,8 +181,8 @@
     tall = jnp.concatenate(
         [jnp.where(first, samp_re, -samp_im), jnp.where(first, samp_im, samp_re)], 0
     )
-    wide = tall.T.astype(jnp.bfloat16)
     tall = tall.astype(jnp.bfloat16)
+    wide = tall.T
     inner = dot(wide[:looks], tall)
 
     half = half_ref[...]
@@ -182,18 +190,17 @@
     near = jnp.concatenate(
         [jnp.where(half >= j, share, 0.0) for j in range(REACH + 1)], axis=0
     )
-    near_hi, near_lo = split(near)
-    seen = dot(near_hi, tall[:dates]) + dot(near_lo, tall[:dates])
-
-    rows_i = lax.broadcasted_iota(jnp.int32, (looks, width), 0)
+    seen = dot(
+        jnp.concatenate(split(near), 1), jnp.concatenate([tall[:dates], tall[:dates]], 0)
+    )
+
     cols_i = lax.broadcasted_iota(jnp.int32, (looks, width), 1)
-    identity = (rows_i == cols_i).astype(jnp.float32)
     turn = jnp.where(cols_i < looks, -1.0, 1.0)
 
     def whole(top):
         return jnp.concatenate([top, turn * pltpu.roll(top, looks, 1)], 0)
 
-    trace = total(inner * identity)
+    trace = total(samp_re * samp_re + samp_im * samp_im) * 0.5
     square = total(inner * inner)
     mean = trace / (looks * dates) + 1e-06
     weight = level_ref[:, :1] / 16.0
@@ -223,8 +230,7 @@
         x, t = x * (2.0 - t), 2.0 * t - t * t
 
     core = (scale * beta) * (m - (mean * scale) * u)
-    core_hi, core_lo = split(core)
-    gain = dot(core_hi, wide) + dot(core_lo, wide)
+    gain = dot(jnp.concatenate(split(core), 1), jnp.concatenate([wide, wide], 0))
     plain = (t - mean * scale * x) * near
     left = gain[:, :dates] + plain
     right = gain[:, dates:]
@@ -396,7 +402,7 @@
         out_specs=(VMEM,) * 7,
         scratch_shapes=[
             pltpu.VMEM((date_local * 16, cols), jnp.float32),
-            pltpu.SemaphoreType.DMA((7,)),
+            pltpu.SemaphoreType.DMA((14,)),
         ],
         interpret=INTERPRET,
         name="fetch",

time: 72.4 us -> 72.5 us (level)
  no operation moved by 1% of the time
where the time goes in v8:
time: 72.5 us; the launch traced here: 72.2 us
  blocking collectives  54.8 us (76%)
  starting transfers between devices  8.02 us (11%)
  Pallas kernels  6.44 us (9%)
  waiting for transfers between devices  2.23 us (3%)
  between operations  0.73 us (1%)
    all_to_all x1, blocking collectives, on_device(): lax.all_to_all(blocks, 'date', split_axis=0, concat_axis=0, tiled=True)  35.8 us
    all_to_all x1, blocking collectives, on_device(): lax.all_to_all(lent, 'date', split_axis=0, concat_axis=0, tiled=True)  18.9 us
    ppermute x1, starting transfers between devices, on_device(): lax.ppermute(far, 'az', swaps([(i, i + 1) for i in range(1, slabs - 1, 2)]))  5.44 us
    pallas_call x1, Pallas kernels, on_device(): pl.pallas_call(link_kernel, out_shape=(chip_out((rows_all, 2 * dates), jn...  2.56 us
    ppermute x1, waiting for transfers between devices, on_device(): lax.ppermute(far, 'az', swaps([(i, i + 1) for i in range(1, slabs - 1, 2)]))  2.23 us
    ppermute x1, starting transfers between devices, on_device(): lax.ppermute(near, 'az', swaps([(i, i + 1) for i in range(0, slabs - 1, 2...  1.92 us
  transfers between devices with their start and end apart: 3, of which 1 were waited for; matrix products, arithmetic and copies ran while one was open for 0% of the time, Pallas kernels for 2%

profile of v8, /device:TPU:40, one launch (start us, length us, event | category | flops | bytes accessed | tf_op | source)
XLA Modules:
  0.0 72.2 jit_solution(16442049903705966381)
XLA Ops:
  0.0 1.4 %fetch.1 = (bf16[2,16,128,128]{3,2,1,0:T(8,128)(2,1)S(1)}, bf16[2,2,16,128]{3,2,1,0:T(8,128)(2,1)S(1)}, bf16[2,2,16,128]{3,2,1,0:T(8,128)(2,1)S(1)}, f32[5,16]{1...) custom-call(bf16[2,16,128,128]{3,2,1,0:T(8,128)(2,1)} %slc_hbm.1, ...), custom_call_target="tpu_custom_call" | custom-call | tf_op jit(solution)/shard_map/fetch/pallas_call | solution.py:393
  1.4 1.9 %collective-permute-start = (bf16[2,2,16,128]{3,2,1,0:T(8,128)(2,1)S(1)}, bf16[2,2,16,128]{3,2,1,0:T(8,128)(2,1)S(1)}, u32[]{:S(2)}, u32[]{:S(2)}) collective-permute-start(bf16[2,2,16,128]{3,2,1,0:T(8,128)(2,1)S(1)} %get-tuple-element.23), channel_id=1, source_target_pairs={{0,1},{1,0},{2,3},{3,2},{4,5},{5,4},{6,7},{7,6},{8,9},{9,8},{10,11... | collective-permute-start | bytes 49160 | tf_op jit(solution)/shard_map/ppermute | solution.py:410
  3.4 5.4 %collective-permute-start.1 = (bf16[2,2,16,128]{3,2,1,0:T(8,128)(2,1)S(1)}, bf16[2,2,16,128]{3,2,1,0:T(8,128)(2,1)S(1)}, u32[]{:S(2)}, u32[]{:S(2)}) collective-permute-start(bf16[2,2,16,128]{3,2,1,0:T(8,128)(2,1)S(1)} %get-tuple-element.24), channel_id=1, source_target_pairs={{1,2},{2,1},{3,4},{4,3},{5,6},{6,5},{7,8},{8,7},{9,10},{10,9},{11,... | collective-permute-start | bytes 49160 | tf_op jit(solution)/shard_map/ppermute | solution.py:411
  9.4 0.9 %azimuth_filter.1 = (bf16[16,2,16,1024]{3,2,1,0:T(8,128)(2,1)S(1)}, f32[2,2,4,16,128]{4,3,2,1,0:T(8,128)S(1)}, f32[1,128]{1,0:T(1,128)S(1)}) custom-call(bf16[2,16,128,128]{3,2,1,0:T(8,128)(2,1)S(1)} %get-tuple-element.19.slc_ref, f32[5,16]{1,0:T(8,128)S(1)} %get-tuple-element.20.taps_ref, s32[1,1]{1,0:T(1,128)S(6)} %copy.11.level_smem), custom_call_target="tpu_custom_call" | custom-call | tf_op jit(solution)/shard_map/azimuth_filter/pallas_call | solution.py:414
  10.4 0.0 collective-permute-done.near_ref
  10.4 2.2 %collective-permute-done.1.far_ref = bf16[2,2,16,128]{3,2,1,0:T(8,128)(2,1)S(1)} collective-permute-done((bf16[2,2,16,128]{3,2,1,0:T(8,128)(2,1)S(1)}, bf16[2,2,16,128]{3,2,1,0:T(8,128)(2,1)S(1)}, u32[]{:S(2)}, u32[]{:S(2)}) %collective-permute-start.1) | collective-permute-done | bytes 16416 | tf_op jit(solution)/shard_map/ppermute | solution.py:411
  12.6 0.2 filter_rim.1
  12.8 35.8 %all_to_all.10.pix_ref = bf16[16,2,16,1024]{3,2,1,0:T(8,128)(2,1)S(1)} all-to-all(bf16[16,2,16,1024]{3,2,1,0:T(8,128)(2,1)S(1)} %filter_rim.1), channel_id=1, replica_groups=mesh['date'=16,'az'=32] {'date'}, dimensions={0} | all-to-all | bytes 2097152 | tf_op jit(solution)/shard_map/all_to_all | solution.py:436
  48.6 2.6 %phase_link.1 = (bf16[192,512]{1,0:T(8,128)(2,1)S(1)}, bf16[4,32,128]{2,1,0:T(8,128)(2,1)S(1)}) custom-call(bf16[16,2,16,1024]{3,2,1,0:T(8,128)(2,1)S(1)} %all_to_all.10.pix_ref, s32[1,64]{1,0:T(1,128)S(1)} %get-tuple-element.25.look_ref, f32[1,128]{1,0:T(1,128)S(1)} %get-tuple-element.26.level_ref, s32[1,256]{1,0:T(1,128)S(1)} %get-tuple-element.27.half_ref, ...), custom_call_target="tpu_custom_call" | custom-call | tf_op jit(solution)/shard_map/phase_link/pallas_call | solution.py:440
  51.2 0.7 collective-permute-start.2
  51.9 0.5 project.1
  52.4 0.0 collective-permute-done.2.edge_ref
  52.4 0.1 pack_rows.1
  52.5 18.9 %all_to_all.11.part_ref = bf16[16,48,128]{2,1,0:T(8,128)(2,1)S(1)} all-to-all(bf16[16,48,128]{2,1,0:T(8,128)(2,1)S(1)} %pack_rows.1), channel_id=1, replica_groups=mesh['date'=16,'az'=32] {'date'}, dimensions={0} | all-to-all | bytes 393216 | tf_op jit(solution)/shard_map/all_to_all | solution.py:483
  71.5 0.8 %overlap_add.1 = f32[2,2,128,128]{3,2,1,0:T(8,128)} custom-call(bf16[16,48,128]{2,1,0:T(8,128)(2,1)S(1)} %all_to_all.11.part_ref), custom_call_target="tpu_custom_call" | custom-call | tf_op jit(solution)/shard_map/overlap_add/pallas_call | solution.py:484
Async XLA Ops:
  1.4 9.0 %collective-permute-start = (bf16[2,2,16,128]{3,2,1,0:T(8,128)(2,1)S(1)}, bf16[2,2,16,128]{3,2,1,0:T(8,128)(2,1)S(1)}, u32[]{:S(2)}, u32[]{:S(2)}) collective-permute-start(bf16[2,2,16,128]{3,2,1,0:T(8,128)(2,1)S(1)} %get-tuple-element.23), channel_id=1, source_target_pairs={{0,1},{1,0},{2,3},{3,2},{4,5},{5,4},{6,7},{7,6},{8,9},{9,8},{10,11... | collective-permute-start | bytes 49160 | tf_op jit(solution)/shard_map/ppermute | solution.py:410
  3.4 9.3 %collective-permute-start.1 = (bf16[2,2,16,128]{3,2,1,0:T(8,128)(2,1)S(1)}, bf16[2,2,16,128]{3,2,1,0:T(8,128)(2,1)S(1)}, u32[]{:S(2)}, u32[]{:S(2)}) collective-permute-start(bf16[2,2,16,128]{3,2,1,0:T(8,128)(2,1)S(1)} %get-tuple-element.24), channel_id=1, source_target_pairs={{1,2},{2,1},{3,4},{4,3},{5,6},{6,5},{7,8},{8,7},{9,10},{10,9},{11,... | collective-permute-start | bytes 49160 | tf_op jit(solution)/shard_map/ppermute | solution.py:411
  51.2 1.2 %collective-permute-start.2 = (bf16[4,32,128]{2,1,0:T(8,128)(2,1)S(1)}, bf16[4,32,128]{2,1,0:T(8,128)(2,1)S(1)}, u32[]{:S(2)}, u32[]{:S(2)}) collective-permute-start(bf16[4,32,128]{2,1,0:T(8,128)(2,1)S(1)} %get-tuple-element.32), channel_id=1, source_target_pairs={{480,481},{481,482},{482,483},{483,484},{484,485},{485,486},{486,4... | collective-permute-start | bytes 98312 | tf_op jit(solution)/shard_map/ppermute | solution.py:451

commit v9 on v8

--- a/solution.py
+++ b/solution.py
@@ -181,8 +181,8 @@
     tall = jnp.concatenate(
         [jnp.where(first, samp_re, -samp_im), jnp.where(first, samp_im, samp_re)], 0
     )
+    wide = tall.T.astype(jnp.bfloat16)
     tall = tall.astype(jnp.bfloat16)
-    wide = tall.T
     inner = dot(wide[:looks], tall)
 
     half = half_ref[...]
@@ -190,9 +190,8 @@
     near = jnp.concatenate(
         [jnp.where(half >= j, share, 0.0) for j in range(REACH + 1)], axis=0
     )
-    seen = dot(
-        jnp.concatenate(split(near), 1), jnp.concatenate([tall[:dates], tall[:dates]], 0)
-    )
+    near_hi, near_lo = split(near)
+    seen = dot(near_hi, tall[:dates]) + dot(near_lo, tall[:dates])
 
     cols_i = lax.broadcasted_iota(jnp.int32, (looks, width), 1)
     turn = jnp.where(cols_i < looks, -1.0, 1.0)
@@ -230,7 +229,8 @@
         x, t = x * (2.0 - t), 2.0 * t - t * t
 
     core = (scale * beta) * (m - (mean * scale) * u)
-    gain = dot(jnp.concatenate(split(core), 1), jnp.concatenate([wide, wide], 0))
+    core_hi, core_lo = split(core)
+    gain = dot(core_hi, wide) + dot(core_lo, wide)
     plain = (t - mean * scale * x) * near
     left = gain[:, :dates] + plain
     right = gain[:, dates:]

time: 72.5 us -> 72.5 us (level)
  no operation moved by 1% of the time
where the time goes in v9:
time: 72.5 us; the launch traced here: 72.3 us
  blocking collectives  54.8 us (76%)
  starting transfers between devices  8.02 us (11%)
  Pallas kernels  6.49 us (9%)
  waiting for transfers between devices  2.23 us (3%)
  between operations  0.73 us (1%)
    all_to_all x1, blocking collectives, on_device(): lax.all_to_all(blocks, 'date', split_axis=0, concat_axis=0, tiled=True)  35.8 us
    all_to_all x1, blocking collectives, on_device(): lax.all_to_all(lent, 'date', split_axis=0, concat_axis=0, tiled=True)  18.9 us
    ppermute x1, starting transfers between devices, on_device(): lax.ppermute(far, 'az', swaps([(i, i + 1) for i in range(1, slabs - 1, 2)]))  5.44 us
    pallas_call x1, Pallas kernels, on_device(): pl.pallas_call(link_kernel, out_shape=(chip_out((rows_all, 2 * dates), jn...  2.6 us
    ppermute x1, waiting for transfers between devices, on_device(): lax.ppermute(far, 'az', swaps([(i, i + 1) for i in range(1, slabs - 1, 2)]))  2.23 us
    ppermute x1, starting transfers between devices, on_device(): lax.ppermute(near, 'az', swaps([(i, i + 1) for i in range(0, slabs - 1, 2...  1.92 us
  transfers between devices with their start and end apart: 3, of which 1 were waited for; matrix products, arithmetic and copies ran while one was open for 0% of the time, Pallas kernels for 2%

profile of v9, /device:TPU:40, one launch (start us, length us, event | category | flops | bytes accessed | tf_op | source)
XLA Modules:
  0.0 72.3 jit_solution(315534474691184521)
XLA Ops:
  0.0 1.4 %fetch.1 = (bf16[2,16,128,128]{3,2,1,0:T(8,128)(2,1)S(1)}, bf16[2,2,16,128]{3,2,1,0:T(8,128)(2,1)S(1)}, bf16[2,2,16,128]{3,2,1,0:T(8,128)(2,1)S(1)}, f32[5,16]{1...) custom-call(bf16[2,16,128,128]{3,2,1,0:T(8,128)(2,1)} %slc_hbm.1, ...), custom_call_target="tpu_custom_call" | custom-call | tf_op jit(solution)/shard_map/fetch/pallas_call | solution.py:393
  1.4 1.9 %collective-permute-start = (bf16[2,2,16,128]{3,2,1,0:T(8,128)(2,1)S(1)}, bf16[2,2,16,128]{3,2,1,0:T(8,128)(2,1)S(1)}, u32[]{:S(2)}, u32[]{:S(2)}) collective-permute-start(bf16[2,2,16,128]{3,2,1,0:T(8,128)(2,1)S(1)} %get-tuple-element.23), channel_id=1, source_target_pairs={{0,1},{1,0},{2,3},{3,2},{4,5},{5,4},{6,7},{7,6},{8,9},{9,8},{10,11... | collective-permute-start | bytes 49160 | tf_op jit(solution)/shard_map/ppermute | solution.py:410
  3.4 5.4 %collective-permute-start.1 = (bf16[2,2,16,128]{3,2,1,0:T(8,128)(2,1)S(1)}, bf16[2,2,16,128]{3,2,1,0:T(8,128)(2,1)S(1)}, u32[]{:S(2)}, u32[]{:S(2)}) collective-permute-start(bf16[2,2,16,128]{3,2,1,0:T(8,128)(2,1)S(1)} %get-tuple-element.24), channel_id=1, source_target_pairs={{1,2},{2,1},{3,4},{4,3},{5,6},{6,5},{7,8},{8,7},{9,10},{10,9},{11,... | collective-permute-start | bytes 49160 | tf_op jit(solution)/shard_map/ppermute | solution.py:411
  9.4 0.9 %azimuth_filter.1 = (bf16[16,2,16,1024]{3,2,1,0:T(8,128)(2,1)S(1)}, f32[2,2,4,16,128]{4,3,2,1,0:T(8,128)S(1)}, f32[1,128]{1,0:T(1,128)S(1)}) custom-call(bf16[2,16,128,128]{3,2,1,0:T(8,128)(2,1)S(1)} %get-tuple-element.19.slc_ref, f32[5,16]{1,0:T(8,128)S(1)} %get-tuple-element.20.taps_ref, s32[1,1]{1,0:T(1,128)S(6)} %copy.11.level_smem), custom_call_target="tpu_custom_call" | custom-call | tf_op jit(solution)/shard_map/azimuth_filter/pallas_call | solution.py:414
  10.4 0.0 collective-permute-done.near_ref
  10.4 2.2 %collective-permute-done.1.far_ref = bf16[2,2,16,128]{3,2,1,0:T(8,128)(2,1)S(1)} collective-permute-done((bf16[2,2,16,128]{3,2,1,0:T(8,128)(2,1)S(1)}, bf16[2,2,16,128]{3,2,1,0:T(8,128)(2,1)S(1)}, u32[]{:S(2)}, u32[]{:S(2)}) %collective-permute-start.1) | collective-permute-done | bytes 16416 | tf_op jit(solution)/shard_map/ppermute | solution.py:411
  12.6 0.2 filter_rim.1
  12.8 35.8 %all_to_all.10.pix_ref = bf16[16,2,16,1024]{3,2,1,0:T(8,128)(2,1)S(1)} all-to-all(bf16[16,2,16,1024]{3,2,1,0:T(8,128)(2,1)S(1)} %filter_rim.1), channel_id=1, replica_groups=mesh['date'=16,'az'=32] {'date'}, dimensions={0} | all-to-all | bytes 2097152 | tf_op jit(solution)/shard_map/all_to_all | solution.py:436
  48.6 2.6 %phase_link.1 = (bf16[192,512]{1,0:T(8,128)(2,1)S(1)}, bf16[4,32,128]{2,1,0:T(8,128)(2,1)S(1)}) custom-call(bf16[16,2,16,1024]{3,2,1,0:T(8,128)(2,1)S(1)} %all_to_all.10.pix_ref, s32[1,64]{1,0:T(1,128)S(1)} %get-tuple-element.25.look_ref, f32[1,128]{1,0:T(1,128)S(1)} %get-tuple-element.26.level_ref, s32[1,256]{1,0:T(1,128)S(1)} %get-tuple-element.27.half_ref, ...), custom_call_target="tpu_custom_call" | custom-call | tf_op jit(solution)/shard_map/phase_link/pallas_call | solution.py:440
  51.2 0.7 collective-permute-start.2
  51.9 0.5 project.1
  52.4 0.0 collective-permute-done.2.edge_ref
  52.5 0.1 pack_rows.1
  52.6 18.9 %all_to_all.11.part_ref = bf16[16,48,128]{2,1,0:T(8,128)(2,1)S(1)} all-to-all(bf16[16,48,128]{2,1,0:T(8,128)(2,1)S(1)} %pack_rows.1), channel_id=1, replica_groups=mesh['date'=16,'az'=32] {'date'}, dimensions={0} | all-to-all | bytes 393216 | tf_op jit(solution)/shard_map/all_to_all | solution.py:483
  71.5 0.8 %overlap_add.1 = f32[2,2,128,128]{3,2,1,0:T(8,128)} custom-call(bf16[16,48,128]{2,1,0:T(8,128)(2,1)S(1)} %all_to_all.11.part_ref), custom_call_target="tpu_custom_call" | custom-call | tf_op jit(solution)/shard_map/overlap_add/pallas_call | solution.py:484
Async XLA Ops:
  1.4 9.0 %collective-permute-start = (bf16[2,2,16,128]{3,2,1,0:T(8,128)(2,1)S(1)}, bf16[2,2,16,128]{3,2,1,0:T(8,128)(2,1)S(1)}, u32[]{:S(2)}, u32[]{:S(2)}) collective-permute-start(bf16[2,2,16,128]{3,2,1,0:T(8,128)(2,1)S(1)} %get-tuple-element.23), channel_id=1, source_target_pairs={{0,1},{1,0},{2,3},{3,2},{4,5},{5,4},{6,7},{7,6},{8,9},{9,8},{10,11... | collective-permute-start | bytes 49160 | tf_op jit(solution)/shard_map/ppermute | solution.py:410
  3.4 9.3 %collective-permute-start.1 = (bf16[2,2,16,128]{3,2,1,0:T(8,128)(2,1)S(1)}, bf16[2,2,16,128]{3,2,1,0:T(8,128)(2,1)S(1)}, u32[]{:S(2)}, u32[]{:S(2)}) collective-permute-start(bf16[2,2,16,128]{3,2,1,0:T(8,128)(2,1)S(1)} %get-tuple-element.24), channel_id=1, source_target_pairs={{1,2},{2,1},{3,4},{4,3},{5,6},{6,5},{7,8},{8,7},{9,10},{10,9},{11,... | collective-permute-start | bytes 49160 | tf_op jit(solution)/shard_map/ppermute | solution.py:411
  51.2 1.2 %collective-permute-start.2 = (bf16[4,32,128]{2,1,0:T(8,128)(2,1)S(1)}, bf16[4,32,128]{2,1,0:T(8,128)(2,1)S(1)}, u32[]{:S(2)}, u32[]{:S(2)}) collective-permute-start(bf16[4,32,128]{2,1,0:T(8,128)(2,1)S(1)} %get-tuple-element.32), channel_id=1, source_target_pairs={{480,481},{481,482},{482,483},{483,484},{484,485},{485,486},{486,4... | collective-permute-start | bytes 98312 | tf_op jit(solution)/shard_map/ppermute | solution.py:451
